TPU v7x, 256 devices: a whole 4x4x8 slice. The times are simulated.
256 devices in a mesh: lon: 32 (over x_lo, z, core), lat: 8 (over x_hi, y).
Axes of the slice: x: 4 (x_hi: 2, x_lo: 2; x = x_hi * 2 + x_lo), y: 4, z: 8, core: 2. Of those that a mesh axis runs over, the one named last changes fastest.
Arguments:
- initial_state: float32 [4, 10, 128, 4096], P(None, None, 'lat', 'lon'), may hold values from -6 to 6
- land_mask: int32 [10, 128, 4096], P(None, 'lat', 'lon'), may hold values from 0 to 1, as said below
- surface_flux: float32 [128, 4096], P('lat', 'lon'), may hold values from 0 to 10, as said below
- weight_in: float32 [40, 64], replicated, may hold values from -1 to 1
- bias_in: float32 [64], replicated, may hold values from -3 to 3
- weight_mid: float32 [64, 64], replicated, may hold values from -0.75 to 0.75
- bias_mid: float32 [64], replicated, may hold values from -3 to 3
- weight_out: float32 [64, 40], replicated, may hold values from -0.75 to 0.75
- bias_out: float32 [40], replicated, may hold values from -3 to 3
- cotangent: float32 [4, 10, 128, 4096], P(None, None, 'lat', 'lon'), may hold values from -6 to 6
Outputs:
- final_state: float32 [4, 10, 128, 4096], P(None, None, 'lat', 'lon')
- state_grad: float32 [4, 10, 128, 4096], P(None, None, 'lat', 'lon')
- grad_weight_in: float32 [40, 64], replicated
- grad_bias_in: float32 [64], replicated
- grad_weight_mid: float32 [64, 64], replicated
- grad_bias_mid: float32 [64], replicated
- grad_weight_out: float32 [64, 40], replicated
- grad_bias_out: float32 [40], replicated
Inputs may be any that keep to these rules, and one draw needn't show every extreme that they name: `land_mask`: at every cell the ocean levels are a run from level 0 down; at least one cell is ocean at every level. `surface_flux`: strictly positive.
All inputs are finite; a program needn't handle non-finite values.
Results may differ from a plain program's by a relative error of at most 0.00012.
Values sent between devices are 32-bit elements; how exact they have to be, the bound alone decides.
A program may use at most 128 MiB of HBM per device.

v0:
```python
import math

import jax
import jax.numpy as jnp
from jax import lax
from jax.sharding import PartitionSpec as P

STEPS = 2


LAT_LIMIT = 1.2
TIME_STEP = 0.25
PRESSURE_GAIN = 0.5
THERMAL_EXPANSION = 0.2
HALINE_CONTRACTION = 0.8
CORIOLIS = 1.0
VISCOSITY = 0.15
DIFFUSIVITY = 0.1
FRESHWATER = 2.0
HIGHEST = lax.Precision.HIGHEST


def padded_2(cells, sides, width):
    for axis, dim in sides:
        count = lax.axis_size(axis)
        head = lax.slice_in_dim(cells, 0, width, axis=dim)
        tail = lax.slice_in_dim(cells, cells.shape[dim] - width, cells.shape[dim], axis=dim)
        cells = jnp.concatenate(
            [
                lax.ppermute(tail, axis, [(i, (i + 1) % count) for i in range(count)]),
                cells,
                lax.ppermute(head, axis, [((i + 1) % count, i) for i in range(count)]),
            ],
            axis=dim,
        )
    return cells


def pressure_of(fields):
    return PRESSURE_GAIN * jnp.cumsum(
        HALINE_CONTRACTION * fields[1] - THERMAL_EXPANSION * fields[0], axis=0
    )


def combine(
    center,
    east_side,
    west_side,
    north_side,
    south_side,
    press_east,
    press_west,
    press_north,
    press_south,
    ocean_cells,
    inv_cos,
    coriolis,
):
    half_metric = 0.5 * inv_cos
    slope_x = (east_side - west_side) * half_metric
    slope_y = (north_side - south_side) * 0.5
    laplace = (east_side + west_side - 2.0 * center) * (inv_cos * inv_cos) + (
        north_side + south_side - 2.0 * center
    )
    along_u = center[2]
    along_v = center[3]
    mixing = jnp.array([DIFFUSIVITY, DIFFUSIVITY, VISCOSITY, VISCOSITY], jnp.float32).reshape(
        (4,) + (1,) * (center.ndim - 1)
    )
    change = mixing * laplace - (along_u * slope_x + along_v * slope_y)
    force_x = coriolis * along_v - (press_east - press_west) * half_metric
    force_y = -coriolis * along_u - (press_north - press_south) * 0.5
    return ocean_cells * jnp.stack([change[0], change[1], change[2] + force_x, change[3] + force_y])


def latitude_terms(row_index, row_count):
    latitude = LAT_LIMIT * (
        2.0 * (jnp.clip(row_index, 0.0, row_count - 1.0) + 0.5) / row_count - 1.0
    )
    return ((1.0 / jnp.cos(latitude))[:, None], (CORIOLIS * jnp.sin(latitude))[:, None])


def tendency(padded, ocean_cells, inv_cos, coriolis):
    pressure = pressure_of(padded)
    return combine(
        padded[..., 1:-1, 1:-1],
        padded[..., 1:-1, 2:],
        padded[..., 1:-1, :-2],
        padded[..., 2:, 1:-1],
        padded[..., :-2, 1:-1],
        pressure[..., 1:-1, 2:],
        pressure[..., 1:-1, :-2],
        pressure[..., 2:, 1:-1],
        pressure[..., :-2, 1:-1],
        ocean_cells,
        inv_cos,
        coriolis,
    )


def fold_back(received, halo_width, row_count, col_count):
    row_band = received[..., 2 * halo_width : 2 * halo_width + row_count, :]
    row_band = row_band.at[..., :halo_width, :].add(received[..., :halo_width, :])
    row_band = row_band.at[..., row_count - halo_width :, :].add(
        received[..., row_count + 3 * halo_width :, :]
    )
    interior = row_band[..., 2 * halo_width : 2 * halo_width + col_count]
    interior = interior.at[..., :halo_width].add(row_band[..., :halo_width])
    return interior.at[..., col_count - halo_width :].add(
        row_band[..., col_count + 3 * halo_width :]
    )


def closure(fields, ocean_cells, weights, forcing):
    weight_in, bias_in, weight_mid, bias_mid, weight_out, bias_out = weights
    columns = fields.reshape(weight_in.shape[0], -1)
    hidden = jnp.tanh(jnp.dot(weight_in.T, columns, precision=HIGHEST) + bias_in[:, None])
    hidden = jnp.tanh(jnp.dot(weight_mid.T, hidden, precision=HIGHEST) + bias_mid[:, None])
    output = (jnp.dot(weight_out.T, hidden, precision=HIGHEST) + bias_out[:, None]).reshape(
        fields.shape
    )
    output = output.at[1, 0].add(forcing)
    return ocean_cells * output


def on_device(
    initial_state,
    land_mask,
    surface_flux,
    weight_in,
    bias_in,
    weight_mid,
    bias_mid,
    weight_out,
    bias_out,
    cotangent,
):
    ocean_cells = land_mask.astype(jnp.float32)
    rows_here = initial_state.shape[2]
    cols_here = initial_state.shape[3]
    lat_total = rows_here * lax.axis_size("lat")
    lon_total = cols_here * lax.axis_size("lon")
    lat_first = lax.axis_index("lat") * rows_here
    weights = (weight_in, bias_in, weight_mid, bias_mid, weight_out, bias_out)
    top_ocean = ocean_cells[0]
    totals = lax.psum((jnp.sum(top_ocean * surface_flux), jnp.sum(top_ocean)), ("lon", "lat"))
    forcing = -FRESHWATER * (surface_flux - totals[0] / totals[1])

    def rows_of(layers):
        return lat_first - layers + jnp.arange(rows_here + 2 * layers, dtype=jnp.int32)

    global_rows = rows_of(1)
    fence_one = ((global_rows >= 0) & (global_rows < lat_total)).astype(jnp.float32)[:, None]
    inv_one, cor_one = latitude_terms(rows_of(0).astype(jnp.float32), lat_total)

    def pad_section(fields):
        return padded_2(fields, (("lon", 3), ("lat", 2)), 1) * fence_one

    def rate_of(padded):
        return tendency(padded, ocean_cells, inv_one, cor_one)

    def advance(fields):
        pad_first = pad_section(fields)
        section_one = fields + TIME_STEP * rate_of(pad_first)
        pad_second = pad_section(section_one)
        section_two = 0.75 * fields + 0.25 * (section_one + TIME_STEP * rate_of(pad_second))
        pad_third = pad_section(section_two)
        section_three = 1.0 / 3.0 * fields + 2.0 / 3.0 * (
            section_two + TIME_STEP * rate_of(pad_third)
        )
        return (section_three, (pad_first, pad_second, pad_third))

    def pull_back(padded, adjoint):
        pullback = jax.vjp(rate_of, padded)[1]
        spread = pullback(adjoint)[0] * fence_one
        received = padded_2(spread, (("lon", 3), ("lat", 2)), 1)
        return fold_back(received, 1, rows_here, cols_here)

    current = ocean_cells * initial_state
    starts = []
    for step_index in range(STEPS):
        starts.append(current)
        advanced, section_pads = advance(current)
        current = advanced + TIME_STEP * closure(current, ocean_cells, weights, forcing)
    adjoint = cotangent
    running = [jnp.zeros_like(item) for item in weights]
    for step_index in reversed(range(STEPS)):
        step_start = starts[step_index]
        section_pads = advance(step_start)[1]
        closure_pullback = jax.vjp(
            lambda fields, params: closure(fields, ocean_cells, params, forcing),
            step_start,
            weights,
        )[1]
        from_closure, weight_terms = closure_pullback(TIME_STEP * adjoint)
        term_win, term_bin, term_wmid, term_bmid, term_wout, term_bout = weight_terms
        running = [
            partial_value + addend
            for partial_value, addend in zip(
                running, (term_win, term_bin, term_wmid, term_bmid, term_wout, term_bout)
            )
        ]
        retreat_pad_first, retreat_pad_second, retreat_pad_third = section_pads
        toward_second = 2.0 / 3.0 * adjoint
        toward_second = toward_second + pull_back(retreat_pad_third, TIME_STEP * toward_second)
        toward_first = 0.25 * toward_second
        toward_first = toward_first + pull_back(retreat_pad_second, TIME_STEP * toward_first)
        toward_start = 1.0 / 3.0 * adjoint + 0.75 * toward_second + toward_first
        adjoint = (
            toward_start + pull_back(retreat_pad_first, TIME_STEP * toward_first) + from_closure
        )
    sum_win, sum_bin, sum_wmid, sum_bmid, sum_wout, sum_bout = running
    summed = lax.psum((sum_win, sum_bin, sum_wmid, sum_bmid, sum_wout, sum_bout), ("lon", "lat"))
    grad_scale = 1.0 / math.sqrt(lat_total * lon_total)
    state_grad = ocean_cells * adjoint
    return (
        current,
        state_grad,
        summed[0] * grad_scale,
        summed[1] * grad_scale,
        summed[2] * grad_scale,
        summed[3] * grad_scale,
        summed[4] * grad_scale,
        summed[5] * grad_scale,
    )


def solution(mesh):
    return jax.shard_map(
        on_device,
        mesh=mesh,
        in_specs=(
            P(None, None, "lat", "lon"),
            P(None, "lat", "lon"),
            P("lat", "lon"),
            P(),
            P(),
            P(),
            P(),
            P(),
            P(),
            P(None, None, "lat", "lon"),
        ),
        out_specs=(
            P(None, None, "lat", "lon"),
            P(None, None, "lat", "lon"),
            P(),
            P(),
            P(),
            P(),
            P(),
            P(),
        ),
        check_vma=False,
    )
```

profile of v0, /device:TPU:24, one launch (start us, length us, event | category | flops | bytes accessed | tf_op | source)
XLA Modules:
  0.0 550.0 jit_solution(14654199477237479227)
XLA Ops:
  2.8 6.3 %collective-permute-start.1 = (f32[4,10,16,1]{3,2,1,0:T(8,128)S(1)}, f32[4,10,16,1]{3,2,1,0:T(8,128)S(1)}, u32[]{:S(2)}, u32[]{:S(2)}) collective-permute-start(f32[4,10,16,1]{3,2,1,0:T(8,128)S(1)} %get-tuple-element.507), channel_id=1, source_target_pairs={{8,0},{16,8},{24,16},{32,24},{40,32},{48,40},{56,48},{64,56},{72,6... | collective-permute-start | bytes 7688 | tf_op jit(solution)/shard_map/ppermute | solution.py:32
  18.3 5.9 %collective-permute-done.3 = f32[4,10,1,130]{3,2,1,0:T(1,128)S(1)} collective-permute-done((f32[4,10,1,130]{3,2,1,0:T(1,128)S(1)}, f32[4,10,1,130]{3,2,1,0:T(1,128)S(1)}, u32[]{:S(2)}, u32[]{:S(2)}) %collective-permute-start.3) | collective-permute-done | bytes 20832 | tf_op jit(solution)/shard_map/ppermute | solution.py:32
  28.0 3.8 collective-permute-start.5
  32.5 4.2 collective-permute-done.4
  50.2 3.8 collective-permute-start.9
  55.3 71.5 %all-reduce.97 = (f32[]{:T(128)}, f32[]{:T(128)}) all-reduce(f32[]{:T(128)} %fusion.198, f32[]{:T(128)} %slice_reduce_fusion), channel_id=1, replica_groups=mesh['lon'=32,'lat'=8] {'lon','lat'}, use_global_device_ids=true, to_apply=%region_4.5 | all-reduce | flops 2 | bytes 16 | tf_op jit(solution)/shard_map/psum | solution.py:146
  135.8 5.9 %collective-permute-done.11 = f32[4,10,1,130]{3,2,1,0:T(1,128)S(1)} collective-permute-done((f32[4,10,1,130]{3,2,1,0:T(1,128)S(1)}, f32[4,10,1,130]{3,2,1,0:T(1,128)S(1)}, u32[]{:S(2)}, u32[]{:S(2)}) %collective-permute-start.11) | collective-permute-done | bytes 20832 | tf_op jit(solution)/shard_map/ppermute | solution.py:32
  147.0 3.8 collective-permute-start.13
  150.8 4.8 collective-permute-done.12
  166.6 4.0 collective-permute-start.17
  170.7 4.6 collective-permute-done.16
  186.4 3.8 collective-permute-start.21
  190.9 4.2 collective-permute-done.20
  209.5 3.8 collective-permute-start.25
  214.0 5.9 %collective-permute-done.24 = f32[4,10,18,1]{3,2,1,0:T(8,128)S(1)} collective-permute-done((f32[4,10,18,1]{3,2,1,0:T(8,128)S(1)}, f32[4,10,18,1]{3,2,1,0:T(8,128)S(1)}, u32[]{:S(2)}, u32[]{:S(2)}) %collective-permute-start.24) | collective-permute-done | bytes 2912 | tf_op jit(solution)/shard_map/ppermute | solution.py:30
  240.4 4.7 scatter-add.95
  254.4 3.8 collective-permute-start.29
  260.3 4.6 collective-permute-done.28
  286.5 4.7 scatter-add.101
  304.4 3.8 collective-permute-start.33
  310.7 4.1 collective-permute-done.32
  336.3 5.1 scatter-add.109
  357.4 76.5 %all-reduce.96 = (f32[40,64]{1,0:T(8,128)}, f32[64]{0:T(128)}, f32[64,64]{1,0:T(8,128)}, f32[64]{0:T(128)}, f32[64,40]{0,1:T(8,128)}, /*index=5*/f32[40]{0:T(128)}) all-reduce(f32[40,64]{1,0:T(8,128)} %convolution_add_fusion.8, f32[64]{0:T(128)} %add.959, ...), channel_id=1, replica_groups=mesh['lon'=32,'lat'=8] {'lon','lat'}, use_global_device_ids=true, to_apply=%region_30.31 | all-reduce | flops 9384 | bytes 75072 | tf_op jit(solution)/shard_map/psum | solution.py:213
  451.4 6.0 %collective-permute-done.36 = f32[4,10,18,1]{3,2,1,0:T(8,128)S(1)} collective-permute-done((f32[4,10,18,1]{3,2,1,0:T(8,128)S(1)}, f32[4,10,18,1]{3,2,1,0:T(8,128)S(1)}, u32[]{:S(2)}, u32[]{:S(2)}) %collective-permute-start.36) | collective-permute-done | bytes 2912 | tf_op jit(solution)/shard_map/ppermute | solution.py:30
  465.4 5.5 %collective-permute-done.39 = f32[4,10,1,132]{3,2,1,0:T(1,128)S(1)} collective-permute-done((f32[4,10,1,132]{3,2,1,0:T(1,128)}, f32[4,10,1,132]{3,2,1,0:T(1,128)S(1)}, u32[]{:S(2)}, u32[]{:S(2)}) %collective-permute-start.39) | collective-permute-done | bytes 21152 | tf_op jit(solution)/shard_map/ppermute | solution.py:32
  478.2 4.0 scatter-add.115
  488.4 3.8 collective-permute-start.41
  492.8 6.1 %collective-permute-done.40 = f32[4,10,18,1]{3,2,1,0:T(8,128)S(1)} collective-permute-done((f32[4,10,18,1]{3,2,1,0:T(8,128)S(1)}, f32[4,10,18,1]{3,2,1,0:T(8,128)S(1)}, u32[]{:S(2)}, u32[]{:S(2)}) %collective-permute-start.40) | collective-permute-done | bytes 2912 | tf_op jit(solution)/shard_map/ppermute | solution.py:30
  522.3 3.8 collective-permute-start.45
  527.4 5.3 collective-permute-done.44
  537.5 4.4 collective-permute-done.47
  543.8 4.0 scatter-add.129
  (586 shorter events, 258.9 us)
Async XLA Ops:
  2.7 11.1 %collective-permute-start = (f32[4,10,16,1]{3,2,1,0:T(8,128)S(1)}, f32[4,10,16,1]{3,2,1,0:T(8,128)S(1)}, u32[]{:S(2)}, u32[]{:S(2)}) collective-permute-start(f32[4,10,16,1]{3,2,1,0:T(8,128)S(1)} %get-tuple-element.506), channel_id=1, source_target_pairs={{0,8},{8,16},{16,24},{24,32},{32,40},{40,48},{48,56},{56,64},{64,7... | collective-permute-start | bytes 7688 | tf_op jit(solution)/shard_map/ppermute | solution.py:30
  2.8 11.0 %collective-permute-start.1 = (f32[4,10,16,1]{3,2,1,0:T(8,128)S(1)}, f32[4,10,16,1]{3,2,1,0:T(8,128)S(1)}, u32[]{:S(2)}, u32[]{:S(2)}) collective-permute-start(f32[4,10,16,1]{3,2,1,0:T(8,128)S(1)} %get-tuple-element.507), channel_id=1, source_target_pairs={{8,0},{16,8},{24,16},{32,24},{40,32},{48,40},{56,48},{64,56},{72,6... | collective-permute-start | bytes 7688 | tf_op jit(solution)/shard_map/ppermute | solution.py:32
  27.9 8.8 %collective-permute-start.4 = (f32[4,10,16,1]{3,2,1,0:T(8,128)S(1)}, f32[4,10,16,1]{3,2,1,0:T(8,128)S(1)}, u32[]{:S(2)}, u32[]{:S(2)}) collective-permute-start(f32[4,10,16,1]{3,2,1,0:T(8,128)S(1)} %get-tuple-element.504), channel_id=1, source_target_pairs={{0,8},{8,16},{16,24},{24,32},{32,40},{40,48},{48,56},{56,64},{64,7... | collective-permute-start | bytes 7688 | tf_op jit(solution)/shard_map/ppermute | solution.py:30
  28.0 8.7 %collective-permute-start.5 = (f32[4,10,16,1]{3,2,1,0:T(8,128)S(1)}, f32[4,10,16,1]{3,2,1,0:T(8,128)S(1)}, u32[]{:S(2)}, u32[]{:S(2)}) collective-permute-start(f32[4,10,16,1]{3,2,1,0:T(8,128)S(1)} %get-tuple-element.505), channel_id=1, source_target_pairs={{8,0},{16,8},{24,16},{32,24},{40,32},{48,40},{56,48},{64,56},{72,6... | collective-permute-start | bytes 7688 | tf_op jit(solution)/shard_map/ppermute | solution.py:32
  37.1 7.7 %collective-permute-start.7 = (f32[4,10,1,130]{3,2,1,0:T(1,128)S(1)}, f32[4,10,1,130]{3,2,1,0:T(1,128)S(1)}, u32[]{:S(2)}, u32[]{:S(2)}) collective-permute-start(f32[4,10,1,130]{3,2,1,0:T(1,128)S(1)} %get-tuple-element.427), channel_id=1, source_target_pairs={{1,0},{2,1},{3,2},{4,3},{5,4},{6,5},{7,6},{0,7},{9,8},{10,9},{11,1... | collective-permute-start | bytes 62408 | tf_op jit(solution)/shard_map/ppermute | solution.py:32
  50.0 79.2 %collective-permute-start.8 = (f32[4,10,16,1]{3,2,1,0:T(8,128)}, f32[4,10,16,1]{3,2,1,0:T(8,128)S(1)}, u32[]{:S(2)}, u32[]{:S(2)}) collective-permute-start(f32[4,10,16,1]{3,2,1,0:T(8,128)} %get-tuple-element.502), channel_id=1, source_target_pairs={{0,8},{8,16},{16,24},{24,32},{32,40},{40,48},{48,56},{56,64},{64,7... | collective-permute-start | bytes 7688 | tf_op jit(solution)/shard_map/ppermute | solution.py:30
  50.2 79.0 %collective-permute-start.9 = (f32[4,10,16,1]{3,2,1,0:T(8,128)}, f32[4,10,16,1]{3,2,1,0:T(8,128)}, u32[]{:S(2)}, u32[]{:S(2)}) collective-permute-start(f32[4,10,16,1]{3,2,1,0:T(8,128)} %get-tuple-element.503), channel_id=1, source_target_pairs={{8,0},{16,8},{24,16},{32,24},{40,32},{48,40},{56,48},{64,56},{72,6... | collective-permute-start | bytes 7688 | tf_op jit(solution)/shard_map/ppermute | solution.py:32
  146.9 8.7 %collective-permute-start.12 = (f32[4,10,16,1]{3,2,1,0:T(8,128)S(1)}, f32[4,10,16,1]{3,2,1,0:T(8,128)S(1)}, u32[]{:S(2)}, u32[]{:S(2)}) collective-permute-start(f32[4,10,16,1]{3,2,1,0:T(8,128)S(1)} %get-tuple-element.500), channel_id=1, source_target_pairs={{0,8},{8,16},{16,24},{24,32},{32,40},{40,48},{48,56},{56,64},{64,7... | collective-permute-start | bytes 7688 | tf_op jit(solution)/shard_map/ppermute | solution.py:30
  147.0 8.6 %collective-permute-start.13 = (f32[4,10,16,1]{3,2,1,0:T(8,128)S(1)}, f32[4,10,16,1]{3,2,1,0:T(8,128)S(1)}, u32[]{:S(2)}, u32[]{:S(2)}) collective-permute-start(f32[4,10,16,1]{3,2,1,0:T(8,128)S(1)} %get-tuple-element.501), channel_id=1, source_target_pairs={{8,0},{16,8},{24,16},{32,24},{40,32},{48,40},{56,48},{64,56},{72,6... | collective-permute-start | bytes 7688 | tf_op jit(solution)/shard_map/ppermute | solution.py:32
  166.5 8.7 %collective-permute-start.16 = (f32[4,10,16,1]{3,2,1,0:T(8,128)S(1)}, f32[4,10,16,1]{3,2,1,0:T(8,128)S(1)}, u32[]{:S(2)}, u32[]{:S(2)}) collective-permute-start(f32[4,10,16,1]{3,2,1,0:T(8,128)S(1)} %get-tuple-element.498), channel_id=1, source_target_pairs={{0,8},{8,16},{16,24},{24,32},{32,40},{40,48},{48,56},{56,64},{64,7... | collective-permute-start | bytes 7688 | tf_op jit(solution)/shard_map/ppermute | solution.py:30
  166.6 8.6 %collective-permute-start.17 = (f32[4,10,16,1]{3,2,1,0:T(8,128)S(1)}, f32[4,10,16,1]{3,2,1,0:T(8,128)S(1)}, u32[]{:S(2)}, u32[]{:S(2)}) collective-permute-start(f32[4,10,16,1]{3,2,1,0:T(8,128)S(1)} %get-tuple-element.499), channel_id=1, source_target_pairs={{8,0},{16,8},{24,16},{32,24},{40,32},{48,40},{56,48},{64,56},{72,6... | collective-permute-start | bytes 7688 | tf_op jit(solution)/shard_map/ppermute | solution.py:32
  175.7 7.7 %collective-permute-start.19 = (f32[4,10,1,130]{3,2,1,0:T(1,128)S(1)}, f32[4,10,1,130]{3,2,1,0:T(1,128)S(1)}, u32[]{:S(2)}, u32[]{:S(2)}) collective-permute-start(f32[4,10,1,130]{3,2,1,0:T(1,128)S(1)} %get-tuple-element.421), channel_id=1, source_target_pairs={{1,0},{2,1},{3,2},{4,3},{5,4},{6,5},{7,6},{0,7},{9,8},{10,9},{11,1... | collective-permute-start | bytes 62408 | tf_op jit(solution)/shard_map/ppermute | solution.py:32
  186.3 8.8 %collective-permute-start.20 = (f32[4,10,16,1]{3,2,1,0:T(8,128)S(1)}, f32[4,10,16,1]{3,2,1,0:T(8,128)S(1)}, u32[]{:S(2)}, u32[]{:S(2)}) collective-permute-start(f32[4,10,16,1]{3,2,1,0:T(8,128)S(1)} %get-tuple-element.496), channel_id=1, source_target_pairs={{0,8},{8,16},{16,24},{24,32},{32,40},{40,48},{48,56},{56,64},{64,7... | collective-permute-start | bytes 7688 | tf_op jit(solution)/shard_map/ppermute | solution.py:30
  186.4 8.7 %collective-permute-start.21 = (f32[4,10,16,1]{3,2,1,0:T(8,128)S(1)}, f32[4,10,16,1]{3,2,1,0:T(8,128)S(1)}, u32[]{:S(2)}, u32[]{:S(2)}) collective-permute-start(f32[4,10,16,1]{3,2,1,0:T(8,128)S(1)} %get-tuple-element.497), channel_id=1, source_target_pairs={{8,0},{16,8},{24,16},{32,24},{40,32},{48,40},{56,48},{64,56},{72,6... | collective-permute-start | bytes 7688 | tf_op jit(solution)/shard_map/ppermute | solution.py:32
  195.5 7.7 %collective-permute-start.23 = (f32[4,10,1,130]{3,2,1,0:T(1,128)S(1)}, f32[4,10,1,130]{3,2,1,0:T(1,128)S(1)}, u32[]{:S(2)}, u32[]{:S(2)}) collective-permute-start(f32[4,10,1,130]{3,2,1,0:T(1,128)S(1)} %get-tuple-element.419), channel_id=1, source_target_pairs={{1,0},{2,1},{3,2},{4,3},{5,4},{6,5},{7,6},{0,7},{9,8},{10,9},{11,1... | collective-permute-start | bytes 62408 | tf_op jit(solution)/shard_map/ppermute | solution.py:32
  209.0 10.9 %collective-permute-start.24 = (f32[4,10,18,1]{3,2,1,0:T(8,128)S(1)}, f32[4,10,18,1]{3,2,1,0:T(8,128)S(1)}, u32[]{:S(2)}, u32[]{:S(2)}) collective-permute-start(f32[4,10,18,1]{3,2,1,0:T(8,128)S(1)} %get-tuple-element.414), channel_id=1, source_target_pairs={{0,8},{8,16},{16,24},{24,32},{32,40},{40,48},{48,56},{56,64},{64,7... | collective-permute-start | bytes 8648 | tf_op jit(solution)/shard_map/ppermute | solution.py:30
  209.5 10.5 %collective-permute-start.25 = (f32[4,10,18,1]{3,2,1,0:T(8,128)S(1)}, f32[4,10,18,1]{3,2,1,0:T(8,128)S(1)}, u32[]{:S(2)}, u32[]{:S(2)}) collective-permute-start(f32[4,10,18,1]{3,2,1,0:T(8,128)S(1)} %get-tuple-element.415), channel_id=1, source_target_pairs={{8,0},{16,8},{24,16},{32,24},{40,32},{48,40},{56,48},{64,56},{72,6... | collective-permute-start | bytes 8648 | tf_op jit(solution)/shard_map/ppermute | solution.py:32
  222.2 7.9 %collective-permute-start.27 = (f32[4,10,1,132]{3,2,1,0:T(1,128)}, f32[4,10,1,132]{3,2,1,0:T(1,128)}, u32[]{:S(2)}, u32[]{:S(2)}) collective-permute-start(f32[4,10,1,132]{3,2,1,0:T(1,128)} %get-tuple-element.379), channel_id=1, source_target_pairs={{1,0},{2,1},{3,2},{4,3},{5,4},{6,5},{7,6},{0,7},{9,8},{10,9},{11,1... | collective-permute-start | bytes 63368 | tf_op jit(solution)/shard_map/ppermute | solution.py:32
  254.3 10.5 %collective-permute-start.28 = (f32[4,10,18,1]{3,2,1,0:T(8,128)S(1)}, f32[4,10,18,1]{3,2,1,0:T(8,128)S(1)}, u32[]{:S(2)}, u32[]{:S(2)}) collective-permute-start(f32[4,10,18,1]{3,2,1,0:T(8,128)S(1)} %get-tuple-element.410), channel_id=1, source_target_pairs={{0,8},{8,16},{16,24},{24,32},{32,40},{40,48},{48,56},{56,64},{64,7... | collective-permute-start | bytes 8648 | tf_op jit(solution)/shard_map/ppermute | solution.py:30
  254.4 10.5 %collective-permute-start.29 = (f32[4,10,18,1]{3,2,1,0:T(8,128)S(1)}, f32[4,10,18,1]{3,2,1,0:T(8,128)S(1)}, u32[]{:S(2)}, u32[]{:S(2)}) collective-permute-start(f32[4,10,18,1]{3,2,1,0:T(8,128)S(1)} %get-tuple-element.411), channel_id=1, source_target_pairs={{8,0},{16,8},{24,16},{32,24},{40,32},{48,40},{56,48},{64,56},{72,6... | collective-permute-start | bytes 8648 | tf_op jit(solution)/shard_map/ppermute | solution.py:32
  268.1 7.9 %collective-permute-start.31 = (f32[4,10,1,132]{3,2,1,0:T(1,128)}, f32[4,10,1,132]{3,2,1,0:T(1,128)}, u32[]{:S(2)}, u32[]{:S(2)}) collective-permute-start(f32[4,10,1,132]{3,2,1,0:T(1,128)} %get-tuple-element.377), channel_id=1, source_target_pairs={{1,0},{2,1},{3,2},{4,3},{5,4},{6,5},{7,6},{0,7},{9,8},{10,9},{11,1... | collective-permute-start | bytes 63368 | tf_op jit(solution)/shard_map/ppermute | solution.py:32
  304.3 10.5 %collective-permute-start.32 = (f32[4,10,18,1]{3,2,1,0:T(8,128)S(1)}, f32[4,10,18,1]{3,2,1,0:T(8,128)S(1)}, u32[]{:S(2)}, u32[]{:S(2)}) collective-permute-start(f32[4,10,18,1]{3,2,1,0:T(8,128)S(1)} %get-tuple-element.406), channel_id=1, source_target_pairs={{0,8},{8,16},{16,24},{24,32},{32,40},{40,48},{48,56},{56,64},{64,7... | collective-permute-start | bytes 8648 | tf_op jit(solution)/shard_map/ppermute | solution.py:30
  304.4 10.5 %collective-permute-start.33 = (f32[4,10,18,1]{3,2,1,0:T(8,128)S(1)}, f32[4,10,18,1]{3,2,1,0:T(8,128)S(1)}, u32[]{:S(2)}, u32[]{:S(2)}) collective-permute-start(f32[4,10,18,1]{3,2,1,0:T(8,128)S(1)} %get-tuple-element.407), channel_id=1, source_target_pairs={{8,0},{16,8},{24,16},{32,24},{40,32},{48,40},{56,48},{64,56},{72,6... | collective-permute-start | bytes 8648 | tf_op jit(solution)/shard_map/ppermute | solution.py:32
  318.0 7.9 %collective-permute-start.35 = (f32[4,10,1,132]{3,2,1,0:T(1,128)}, f32[4,10,1,132]{3,2,1,0:T(1,128)}, u32[]{:S(2)}, u32[]{:S(2)}) collective-permute-start(f32[4,10,1,132]{3,2,1,0:T(1,128)} %get-tuple-element.375), channel_id=1, source_target_pairs={{1,0},{2,1},{3,2},{4,3},{5,4},{6,5},{7,6},{0,7},{9,8},{10,9},{11,1... | collective-permute-start | bytes 63368 | tf_op jit(solution)/shard_map/ppermute | solution.py:32
  446.9 10.4 %collective-permute-start.36 = (f32[4,10,18,1]{3,2,1,0:T(8,128)S(1)}, f32[4,10,18,1]{3,2,1,0:T(8,128)S(1)}, u32[]{:S(2)}, u32[]{:S(2)}) collective-permute-start(f32[4,10,18,1]{3,2,1,0:T(8,128)S(1)} %get-tuple-element.402), channel_id=1, source_target_pairs={{0,8},{8,16},{16,24},{24,32},{32,40},{40,48},{48,56},{56,64},{64,7... | collective-permute-start | bytes 8648 | tf_op jit(solution)/shard_map/ppermute | solution.py:30
  447.0 10.3 %collective-permute-start.37 = (f32[4,10,18,1]{3,2,1,0:T(8,128)S(1)}, f32[4,10,18,1]{3,2,1,0:T(8,128)S(1)}, u32[]{:S(2)}, u32[]{:S(2)}) collective-permute-start(f32[4,10,18,1]{3,2,1,0:T(8,128)S(1)} %get-tuple-element.403), channel_id=1, source_target_pairs={{8,0},{16,8},{24,16},{32,24},{40,32},{48,40},{56,48},{64,56},{72,6... | collective-permute-start | bytes 8648 | tf_op jit(solution)/shard_map/ppermute | solution.py:32
  463.1 7.8 %collective-permute-start.39 = (f32[4,10,1,132]{3,2,1,0:T(1,128)}, f32[4,10,1,132]{3,2,1,0:T(1,128)S(1)}, u32[]{:S(2)}, u32[]{:S(2)}) collective-permute-start(f32[4,10,1,132]{3,2,1,0:T(1,128)} %get-tuple-element.373), channel_id=1, source_target_pairs={{1,0},{2,1},{3,2},{4,3},{5,4},{6,5},{7,6},{0,7},{9,8},{10,9},{11,1... | collective-permute-start | bytes 63368 | tf_op jit(solution)/shard_map/ppermute | solution.py:32
  488.3 10.5 %collective-permute-start.40 = (f32[4,10,18,1]{3,2,1,0:T(8,128)S(1)}, f32[4,10,18,1]{3,2,1,0:T(8,128)S(1)}, u32[]{:S(2)}, u32[]{:S(2)}) collective-permute-start(f32[4,10,18,1]{3,2,1,0:T(8,128)S(1)} %get-tuple-element.398), channel_id=1, source_target_pairs={{0,8},{8,16},{16,24},{24,32},{32,40},{40,48},{48,56},{56,64},{64,7... | collective-permute-start | bytes 8648 | tf_op jit(solution)/shard_map/ppermute | solution.py:30
  488.4 10.4 %collective-permute-start.41 = (f32[4,10,18,1]{3,2,1,0:T(8,128)S(1)}, f32[4,10,18,1]{3,2,1,0:T(8,128)S(1)}, u32[]{:S(2)}, u32[]{:S(2)}) collective-permute-start(f32[4,10,18,1]{3,2,1,0:T(8,128)S(1)} %get-tuple-element.399), channel_id=1, source_target_pairs={{8,0},{16,8},{24,16},{32,24},{40,32},{48,40},{56,48},{64,56},{72,6... | collective-permute-start | bytes 8648 | tf_op jit(solution)/shard_map/ppermute | solution.py:32
  522.0 10.8 %collective-permute-start.44 = (f32[4,10,18,1]{3,2,1,0:T(8,128)S(1)}, f32[4,10,18,1]{3,2,1,0:T(8,128)S(1)}, u32[]{:S(2)}, u32[]{:S(2)}) collective-permute-start(f32[4,10,18,1]{3,2,1,0:T(8,128)S(1)} %get-tuple-element.394), channel_id=1, source_target_pairs={{0,8},{8,16},{16,24},{24,32},{32,40},{40,48},{48,56},{56,64},{64,7... | collective-permute-start | bytes 8648 | tf_op jit(solution)/shard_map/ppermute | solution.py:30
  522.3 10.5 %collective-permute-start.45 = (f32[4,10,18,1]{3,2,1,0:T(8,128)S(1)}, f32[4,10,18,1]{3,2,1,0:T(8,128)S(1)}, u32[]{:S(2)}, u32[]{:S(2)}) collective-permute-start(f32[4,10,18,1]{3,2,1,0:T(8,128)S(1)} %get-tuple-element.395), channel_id=1, source_target_pairs={{8,0},{16,8},{24,16},{32,24},{40,32},{48,40},{56,48},{64,56},{72,6... | collective-permute-start | bytes 8648 | tf_op jit(solution)/shard_map/ppermute | solution.py:32
  534.2 7.7 %collective-permute-start.47 = (f32[4,10,1,132]{3,2,1,0:T(1,128)S(1)}, f32[4,10,1,132]{3,2,1,0:T(1,128)S(1)}, u32[]{:S(2)}, u32[]{:S(2)}) collective-permute-start(f32[4,10,1,132]{3,2,1,0:T(1,128)S(1)} %get-tuple-element.369), channel_id=1, source_target_pairs={{1,0},{2,1},{3,2},{4,3},{5,4},{6,5},{7,6},{0,7},{9,8},{10,9},{11,1... | collective-permute-start | bytes 63368 | tf_op jit(solution)/shard_map/ppermute | solution.py:32
  (157 other events, 689.9 us)
where the time goes:
time: 561 us; the launch traced here: 550 us
  blocking collectives  148 us (26%)
  waiting for transfers between devices  113 us (20%)
  local copies, waits for them, and re-layouts  108 us (19%)
  other arithmetic  81 us (14%)
  starting transfers between devices  78.5 us (14%)
  matrix products  17.7 us (3%)
    psum x1, blocking collectives, on_device(): lax.psum((sum_win, sum_bin, sum_wmid, sum_bmid, sum_wout, sum_bout), ('lo...  76.5 us
    psum x1, blocking collectives, on_device(): lax.psum((jnp.sum(top_ocean * surface_flux), jnp.sum(top_ocean)), ('lon',...  71.5 us
    ppermute x24, starting transfers between devices, padded_2(): lax.ppermute(head, axis, [((i + 1) % count, i) for i in range(count)])  64.4 us
    ppermute x24, waiting for transfers between devices, padded_2(): lax.ppermute(tail, axis, [(i, (i + 1) % count) for i in range(count)])  63.4 us
    ppermute x24, waiting for transfers between devices, padded_2(): lax.ppermute(head, axis, [((i + 1) % count, i) for i in range(count)])  49.6 us
    unnamed x286, local copies, waits for them, and re-layouts  32.5 us
    scatter-add x6, local copies, waits for them, and re-layouts, fold_back(): interior.at[..., col_count - halo_width:]  25.4 us
    ppermute x24, starting transfers between devices, padded_2(): lax.ppermute(tail, axis, [(i, (i + 1) % count) for i in range(count)])  14.1 us
  transfers between devices with their start and end apart: 48, of which 35 were waited for; matrix products, arithmetic and copies ran while one was open for 7% of the time, Pallas kernels for 0%

commit v1 on v0

v1 whole, which is shorter than its diff:
```python
import functools
import math

import jax
import jax.numpy as jnp
from jax import lax
from jax.experimental import pallas as pl
from jax.experimental.pallas import tpu as pltpu
from jax.sharding import PartitionSpec as P

F32 = jnp.float32
BF16 = jnp.bfloat16
MESH = pl.DeviceIdType.MESH

LEV = 10
FEAT = 40
HID = 64
ROWS = 16
COLS = 128
CELLS = ROWS * COLS
PAD = 32

LAT_LIMIT = 1.2
DT = 0.25
MIX = (0.1, 0.1, 0.15, 0.15)
GAIN_S = 0.5 * 0.8
GAIN_T = -0.5 * 0.2
FRESHWATER = 2.0
CHUNK = 512


def split(x):
    hi = x.astype(BF16)
    lo = (x - hi.astype(F32)).astype(BF16)
    return hi, lo


def kernel(
    lat_count,
    lon_count,
    state,
    mask,
    flux,
    win,
    b_in,
    wmid,
    b_mid,
    wout,
    b_out,
    cot,
    fin,
    grad,
    g_win,
    g_bin,
    g_wmid,
    g_bmid,
    g_wout,
    g_bout,
    xs,
    ew,
    ns,
    pe,
    mw,
    pn,
    mn,
    acc,
    lam,
    t2,
    t1,
    zc,
    h1,
    h2,
    dout,
    da2,
    da1,
    mx,
    dx,
    dox,
    lhs,
    bcol,
    square,
    gb,
    rs1,
    c1,
    rs2,
    c2,
    ag,
    f0,
    fr1,
    f1,
    fr2,
    row_s,
    row_r,
    col_s,
    col_r,
    h_send,
    h_recv,
    a_send,
    a_recv,
):
    lon = lax.axis_index("lon")
    lat = lax.axis_index("lat")
    east = lax.rem(lon + 1, lon_count)
    west = lax.rem(lon + lon_count - 1, lon_count)
    has_n = lat < lat_count - 1
    has_s = lat > 0
    halves = 2
    near = lon_count // halves
    far = lat_count * halves
    share = 128 // near
    half = lon // near
    spot = lon - half * near
    other = lat * halves + half

    def along(d):
        return {"lon": half * near + lax.rem(spot + d, near), "lat": lat}

    def across(d):
        to = lax.rem(other + d, far)
        to_lat = to // halves
        return {"lon": (to - to_lat * halves) * near + spot, "lat": to_lat}

    north_id = {"lon": lon, "lat": lat + 1}
    south_id = {"lon": lon, "lat": lat - 1}
    east_id = {"lon": east, "lat": lat}
    west_id = {"lon": west, "lat": lat}

    barrier = pltpu.get_barrier_semaphore()

    def greet(to):
        pl.semaphore_signal(barrier, inc=1, device_id=to, device_id_type=MESH)

    greet(east_id)
    greet(west_id)

    @pl.when(has_n)
    def _():
        greet(north_id)

    @pl.when(has_s)
    def _():
        greet(south_id)

    for d in range(1, near):
        greet(along(d))
    for d in range(1, far):
        greet(across(d))

    lane = lax.broadcasted_iota(jnp.int32, (ROWS, COLS), 1)
    row = lax.broadcasted_iota(jnp.int32, (ROWS, COLS), 0)
    first_lane = lane == 0
    last_lane = lane == COLS - 1
    odd_lane = lax.rem(lane, 2) == 1
    low_lane = lane < 64
    grow = (row + lat * ROWS).astype(F32)
    phi = LAT_LIMIT * (2.0 * (grow + 0.5) / (lat_count * ROWS) - 1.0)
    sq = phi * phi
    cosine = jnp.ones_like(phi)
    sine = jnp.ones_like(phi)
    for n in range(8, 0, -1):
        cosine = 1.0 - cosine * sq * (1.0 / ((2 * n - 1) * (2 * n)))
        sine = 1.0 - sine * sq * (1.0 / ((2 * n) * (2 * n + 1)))
    inv_cos = 1.0 / cosine
    cor = sine * phi
    hm = 0.5 * inv_cos
    cc = inv_cos * inv_cos
    depth = mask[0]
    for l in range(1, LEV):
        depth = depth + mask[l]

    def hcopy(e, d):
        if d == 0:
            src, dst, to = row_s.at[e, 0], row_r.at[e, 0], north_id
        elif d == 1:
            src, dst, to = row_s.at[e, 1], row_r.at[e, 1], south_id
        elif d == 2:
            src, dst, to = col_s.at[e], col_r.at[e, 0], east_id
        else:
            src, dst, to = col_s.at[e], col_r.at[e, 1], west_id
        return pltpu.make_async_remote_copy(
            src_ref=src,
            dst_ref=dst,
            send_sem=h_send.at[e, d],
            recv_sem=h_recv.at[e, d],
            device_id=to,
            device_id_type=MESH,
        )

    def launch(e):
        @pl.when(has_n)
        def _():
            hcopy(e, 0).start()

        @pl.when(has_s)
        def _():
            hcopy(e, 1).start()

        hcopy(e, 2).start()
        hcopy(e, 3).start()

    def arrive(e):
        @pl.when(has_s)
        def _():
            hcopy(e, 0).wait_recv()

        @pl.when(has_n)
        def _():
            hcopy(e, 1).wait_recv()

        hcopy(e, 2).wait_recv()
        hcopy(e, 3).wait_recv()

    def drain(e):
        @pl.when(has_n)
        def _():
            hcopy(e, 0).wait_send()

        @pl.when(has_s)
        def _():
            hcopy(e, 1).wait_send()

        hcopy(e, 2).wait_send()
        hcopy(e, 3).wait_send()

    def take_rows(ref, r, count):
        return ref.reshape(FEAT * count, COLS)[pl.ds(r, FEAT, stride=count), :]

    def put_rows(ref, r, count, value):
        ref.reshape(FEAT * count, COLS)[pl.ds(r, FEAT, stride=count), :] = value

    def pack(packed, value, fl):
        turned = pltpu.roll(value, 2 * fl + 1, 1)
        return jnp.where(lane // 2 == fl, turned, packed)

    def part(at):
        return pl.ds(pl.multiple_of(at * share, share), share)

    def others(stage):
        return range(1, far if stage in (1, 3) else near)

    def fan(stage, d, src, dst, to):
        return pltpu.make_async_remote_copy(
            src_ref=src,
            dst_ref=dst,
            send_sem=a_send.at[stage, d],
            recv_sem=a_recv.at[stage, d],
            device_id=to,
            device_id_type=MESH,
        )

    def fan_copy(stage, d):
        if stage == 0:
            return fan(stage, d, f0, fr1.at[d], along(d))
        if stage == 1:
            return fan(stage, d, f1, fr2.at[d], across(d))
        if stage == 2:
            return fan(stage, d, gb.at[part(lax.rem(spot + d, near))], rs1.at[d], along(d))
        if stage == 3:
            return fan(stage, d, c1, rs2.at[d], across(d))
        return fan(stage, d, c2, ag.at[part(spot)], along(d))

    def fan_start(stage):
        for d in others(stage):
            fan_copy(stage, d).start()

    def fan_arrive(stage):
        for d in others(stage):
            fan_copy(stage, d).wait_recv()

    def fan_drain(stage):
        for d in others(stage):
            fan_copy(stage, d).wait_send()

    def slot_sum(stage, own, slots):
        total = own
        for d in others(stage):
            total = total + slots[d]
        return total

    def begin(l, packed):
        wet = depth > l
        for f in range(4):
            fl = f * LEV + l
            x = jnp.where(wet, state[fl], 0.0)
            xs[0, fl, 8:24, :] = x
            packed = pack(packed, x, fl)
        return packed

    blank = jnp.zeros((ROWS, COLS), F32)
    packed = lax.fori_loop(0, LEV, begin, blank)
    col_s[0] = packed

    def stage_rows(e, north_ref, south_ref):
        row_s[e, 0] = take_rows(north_ref, 23, PAD)
        row_s[e, 1] = take_rows(south_ref, 8, PAD)

    stage_rows(0, xs.at[0], xs.at[0])
    wet_top = depth > 0
    part_flux = jnp.sum(jnp.where(wet_top, flux[...], 0.0), axis=0, keepdims=True)
    part_count = jnp.sum(jnp.where(wet_top, 1.0, 0.0), axis=0, keepdims=True)
    row8 = lax.broadcasted_iota(jnp.int32, (8, COLS), 0)
    f0[...] = jnp.where(
        row8 == 0,
        jnp.broadcast_to(part_flux, (8, COLS)),
        jnp.where(row8 == 1, jnp.broadcast_to(part_count, (8, COLS)), 0.0),
    )

    meet = near + far + has_n.astype(jnp.int32) + has_s.astype(jnp.int32)
    pl.semaphore_wait(barrier, meet)
    launch(0)
    fan_start(0)

    @pl.when(jnp.logical_not(has_s))
    def _():
        for e in range(12):
            row_r[e, 0] = jnp.zeros((FEAT, COLS), F32)

    @pl.when(jnp.logical_not(has_n))
    def _():
        for e in range(12):
            row_r[e, 1] = jnp.zeros((FEAT, COLS), F32)

    def weight(at, value):
        hi, lo = split(value)
        lhs[at, :, 0:64] = hi
        lhs[at, :, 64:128] = hi
        lhs[at, :, 128:192] = lo

    def both(value_ref, rows, cols, plain, turned):
        square[...] = jnp.zeros((COLS, COLS), F32)
        square[0:rows, 0:cols] = value_ref[...]
        whole = square[...]
        weight(plain, whole[0:64, 0:64])
        weight(turned, whole.T[0:64, 0:64])

    def prepare():
        both(wout, HID, FEAT, 3, 2)
        both(wmid, HID, HID, 4, 1)
        both(win, FEAT, HID, 5, 0)
        square[...] = jnp.zeros((COLS, COLS), F32)
        square[0:1, 0:HID] = b_in[...]
        square[1:2, 0:HID] = b_mid[...]
        square[2:3, 0:FEAT] = b_out[...]
        turned = square[...].T
        for at in range(3):
            bcol[at] = jnp.broadcast_to(turned[0:64, at : at + 1], (64, COLS))
        for s in range(2):
            zc[s, FEAT:64, :] = jnp.zeros((64 - FEAT, CELLS), F32)
        dout[FEAT:64, :] = jnp.zeros((64 - FEAT, CELLS), F32)
        gb[112:128] = jnp.zeros((16, COLS), F32)

    def product(at, x):
        hi, lo = split(x)
        return jnp.dot(
            lhs[at], jnp.concatenate([hi, lo, hi], axis=0), preferred_element_type=F32
        )

    def bias(at):
        return jnp.concatenate([bcol[at]] * (CHUNK // COLS), axis=1)

    def gather(ref, first, count, out):
        for r in range(ROWS):
            out[0:FEAT, r * COLS : (r + 1) * COLS] = take_rows(ref, first + r, count)

    chunks = [pl.ds(c * CHUNK, CHUNK) for c in range(CELLS // CHUNK)]

    def layer_one(s):
        gather(xs.at[3 * s], 8, PAD, zc.at[s])
        for c in chunks:
            h1[s, :, c] = jnp.tanh(product(0, zc[s, :, c]) + bias(0))

    def layer_two(s):
        for c in chunks:
            h2[s, :, c] = jnp.tanh(product(1, h1[s, :, c]) + bias(1))

    def scatter(ref, n, value):
        for j in range(CHUNK // COLS):
            put_rows(
                ref, n * (CHUNK // COLS) + j, ROWS, value[0:FEAT, j * COLS : (j + 1) * COLS]
            )

    def layer_three(s):
        for n, c in enumerate(chunks):
            scatter(mx, n, product(2, h2[s, :, c]) + bias(2))

    def back_out(s, source):
        def body(l, carry):
            wet = depth > l
            for f in range(4):
                fl = f * LEV + l
                dox[fl] = jnp.where(wet, DT * source[fl], 0.0)
            return carry

        lax.fori_loop(0, LEV, body, 0)
        gather(dox, 0, ROWS, dout)
        for c in chunks:
            h = h2[s, :, c]
            da2[:, c] = product(3, dout[:, c]) * (1.0 - h * h)

    def back_mid(s):
        for c in chunks:
            h = h1[s, :, c]
            da1[:, c] = product(4, da2[:, c]) * (1.0 - h * h)

    def back_in(s):
        for n, c in enumerate(chunks):
            scatter(dx, n, product(5, da1[:, c]))

    def outer(left_ref, right_ref):
        total = jnp.zeros((144, COLS), F32)
        ones = jnp.ones((16, CHUNK), BF16)
        for c in chunks:
            hi, lo = split(left_ref[:, c])
            r_hi, r_lo = split(right_ref[:, c])
            total = total + lax.dot_general(
                jnp.concatenate([hi, lo, ones], axis=0),
                jnp.concatenate([r_hi, r_lo], axis=0),
                (((1,), (1,)), ((), ())),
                preferred_element_type=F32,
            )
        folded = total + pltpu.roll(total, 64, 1)
        return folded[0:64] + total[64:128], folded[128:136]

    def weight_grads(s, add):
        g_in, s_in = outer(zc.at[s], da1)
        g_mid, s_mid = outer(h1.at[s], da2)
        g_out, s_out = outer(h2.at[s], dout)
        wide = lax.broadcasted_iota(jnp.int32, (64, COLS), 1) < 64
        low8 = lax.broadcasted_iota(jnp.int32, (8, COLS), 1) < 64
        top = jnp.where(wide, g_mid, pltpu.roll(g_out, 64, 1))
        low = jnp.where(wide, g_in, 0.0)[0:FEAT]
        sums = jnp.where(
            row8 == 0, s_in, jnp.where(row8 == 1, s_mid, jnp.where(row8 == 2, s_out, 0.0))
        )
        sums = jnp.where(low8, sums, 0.0)
        if add:
            gb[0:64] = gb[0:64] + top
            gb[64:104] = gb[64:104] + low
            gb[104:112] = gb[104:112] + sums
        else:
            gb[0:64] = top
            gb[64:104] = low
            gb[104:112] = sums

    def sides(turned, q_west, q_east):
        w_side = pltpu.roll(jnp.where(last_lane, turned, q_west), 1, 1)
        e_side = pltpu.roll(jnp.where(first_lane, turned, q_east), COLS - 1, 1)
        return w_side, e_side

    def halo(e):
        return jnp.where(odd_lane, col_r[e, 1], col_r[e, 0])

    def turn(packed, fl):
        return pltpu.roll(packed, lax.rem(2 * COLS - 1 - 2 * fl, COLS), 1)

    def forward(k, forcing):
        start, stage = 3 * (k // 3), k % 3
        arrive(k)
        put_rows(xs.at[k], 7, PAD, row_r[k, 0])
        put_rows(xs.at[k], 24, PAD, row_r[k, 1])
        received = halo(k)

        def body(l, carry):
            packed, press_x, press_y = carry
            wet = depth > l
            u = xs[k, 2 * LEV + l, 8:24, :]
            v = xs[k, 3 * LEV + l, 8:24, :]
            uh = u * hm
            vh = v * 0.5
            for f in range(4):
                fl = f * LEV + l
                q = xs[k, fl, 8:24, :]
                north = xs[k, fl, 9:25, :]
                south = xs[k, fl, 7:23, :]
                w_side, e_side = sides(turn(received, fl), q, q)
                d_x = e_side - w_side
                d_y = north - south
                ew[k, fl] = d_x
                ns[k, fl] = d_y
                mix = MIX[f]
                change = (
                    (mix * cc) * (e_side + w_side - 2.0 * q)
                    + mix * (north + south - 2.0 * q)
                    - (uh * d_x + vh * d_y)
                )
                if f == 0:
                    press_x = press_x + GAIN_T * d_x
                    press_y = press_y + GAIN_T * d_y
                if f == 1:
                    press_x = press_x + GAIN_S * d_x
                    press_y = press_y + GAIN_S * d_y
                if f == 2:
                    change = change + (cor * v - press_x * hm)
                if f == 3:
                    change = change - (cor * u + press_y * 0.5)
                moved = q + jnp.where(wet, DT * change, 0.0)
                if stage == 0:
                    new = moved
                elif stage == 1:
                    new = 0.75 * xs[start, fl, 8:24, :] + 0.25 * moved
                else:
                    given = mx[fl]
                    if f == 1:
                        given = given + jnp.where(l == 0, forcing, 0.0)
                    new = (
                        (1.0 / 3.0) * xs[start, fl, 8:24, :]
                        + (2.0 / 3.0) * moved
                        + jnp.where(wet, DT * given, 0.0)
                    )
                if k < 5:
                    xs[k + 1, fl, 8:24, :] = new
                    packed = pack(packed, new, fl)
                else:
                    fin[fl] = new
            return packed, press_x, press_y

        packed, _, _ = lax.fori_loop(0, LEV, body, (blank, blank, blank))
        if k < 5:
            col_s[k + 1] = packed
            stage_rows(k + 1, xs.at[k + 1], xs.at[k + 1])
            launch(k + 1)

    def give(n, source):
        k, stage = 5 - n, (5 - n) % 3
        scale = (1.0, 0.25, 2.0 / 3.0)[stage]

        def body(t, carry):
            packed, sum_u, sum_v = carry
            l = LEV - 1 - t
            wet = depth > l
            g = [jnp.where(wet, (DT * scale) * source[f * LEV + l], 0.0) for f in range(4)]
            sum_u = sum_u + g[2]
            sum_v = sum_v + g[3]
            u = xs[k, 2 * LEV + l, 8:24, :]
            v = xs[k, 3 * LEV + l, 8:24, :]
            uh = u * hm
            vh = v * 0.5
            push_x = hm * sum_u
            push_y = 0.5 * sum_v
            to_u = cor * g[3]
            to_v = cor * g[2]
            for f in range(4):
                fl = f * LEV + l
                mix = MIX[f]
                a = uh * g[f]
                b = vh * g[f]
                if f == 0:
                    a = a + GAIN_T * push_x
                    b = b + GAIN_T * push_y
                if f == 1:
                    a = a + GAIN_S * push_x
                    b = b + GAIN_S * push_y
                base = (mix * cc) * g[f]
                plus = base + a
                minus = base - a
                flat = mix * g[f]
                pe[fl] = plus
                mw[fl] = minus
                pn[fl, 8:24, :] = flat + b
                mn[fl, 8:24, :] = flat - b
                packed = pack(packed, jnp.where(low_lane, plus, minus), fl)
                to_u = to_u + g[f] * (hm * ew[k, fl])
                to_v = to_v - g[f] * (0.5 * ns[k, fl])
            for f in range(4):
                fl = f * LEV + l
                own = -2.0 * (MIX[f] * cc + MIX[f]) * g[f]
                if f == 2:
                    own = own - to_u
                if f == 3:
                    own = own + to_v
                acc[fl] = own
            return packed, sum_u, sum_v

        packed, _, _ = lax.fori_loop(0, LEV, body, (blank, blank, blank))
        col_s[6 + n] = packed
        stage_rows(6 + n, mn, pn)
        launch(6 + n)

    def take(n, source):
        stage = (5 - n) % 3
        e = 6 + n
        arrive(e)
        put_rows(mn, 7, PAD, row_r[e, 0])
        put_rows(pn, 24, PAD, row_r[e, 1])
        received = halo(e)

        def body(l, carry):
            for f in range(4):
                fl = f * LEV + l
                w_side, e_side = sides(turn(received, fl), mw[fl], pe[fl])
                got = acc[fl] + w_side + e_side + pn[fl, 9:25, :] + mn[fl, 7:23, :]
                if stage == 2:
                    t2[fl] = (2.0 / 3.0) * source[fl] + got
                elif stage == 1:
                    t1[fl] = 0.25 * t2[fl] + got
                else:
                    new = (1.0 / 3.0) * source[fl] + 0.75 * t2[fl] + t1[fl] + got + dx[fl]
                    if n == 5:
                        grad[fl] = jnp.where(depth > l, new, 0.0)
                    else:
                        lam[fl] = new
            return carry

        lax.fori_loop(0, LEV, body, 0)

    prepare()
    layer_one(0)
    forward(0, None)
    fan_arrive(0)
    f1[...] = slot_sum(0, f0[...], fr1)
    fan_start(1)
    layer_two(0)
    forward(1, None)
    layer_three(0)
    fan_arrive(1)
    totals = slot_sum(1, f1[...], fr2)
    flux_sum = jnp.sum(totals[0:1, :], axis=1, keepdims=True)
    count_sum = jnp.sum(totals[1:2, :], axis=1, keepdims=True)
    mean = jnp.broadcast_to(flux_sum / count_sum, (ROWS, COLS))
    forcing = -FRESHWATER * (flux[...] - mean)
    forward(2, forcing)
    layer_one(1)
    forward(3, None)
    layer_two(1)
    forward(4, None)
    layer_three(1)
    forward(5, forcing)

    give(0, cot)
    back_out(1, cot)
    take(0, cot)
    give(1, t2)
    back_mid(1)
    back_in(1)
    take(1, cot)
    give(2, t1)
    weight_grads(1, False)
    take(2, cot)
    give(3, lam)
    back_out(0, lam)
    back_mid(0)
    take(3, lam)
    give(4, t2)
    weight_grads(0, True)
    fan_start(2)
    back_in(0)
    take(4, lam)
    give(5, t1)
    fan_arrive(2)
    c1[...] = slot_sum(2, gb[part(spot)], rs1)
    fan_start(3)
    take(5, lam)
    fan_arrive(3)
    scale = 1.0 / math.sqrt(lat_count * ROWS * lon_count * COLS)
    c2[...] = slot_sum(3, c1[...], rs2) * scale
    ag[part(spot)] = c2[...]
    fan_start(4)
    for e in range(12):
        drain(e)
    for stage in range(4):
        fan_drain(stage)
    fan_arrive(4)
    top = ag[0:64]
    g_wmid[...] = top[:, 0:HID]
    g_wout[...] = pltpu.roll(top, 64, 1)[:, 0:FEAT]
    g_win[...] = ag[64:104][:, 0:HID]
    sums = ag[104:112]
    g_bin[...] = sums[0:1, 0:HID]
    g_bmid[...] = sums[1:2, 0:HID]
    g_bout[...] = sums[2:3, 0:FEAT]
    fan_drain(4)


def on_device(lat_count, lon_count, state, mask, flux, win, b_in, wmid, b_mid, wout, b_out, cot):
    def v(*shape):
        return pltpu.VMEM(shape, F32)

    near, far = lon_count // 2, lat_count * 2
    share = 128 // near
    vmem = pl.BlockSpec(memory_space=pltpu.VMEM)
    field = (FEAT, ROWS, COLS)
    tall = (FEAT, PAD, COLS)
    wide = (64, CELLS)
    out = pl.pallas_call(
        functools.partial(kernel, lat_count, lon_count),
        out_shape=[
            jax.ShapeDtypeStruct(shape, F32)
            for shape in (
                field,
                field,
                (FEAT, HID),
                (1, HID),
                (HID, HID),
                (1, HID),
                (HID, FEAT),
                (1, FEAT),
            )
        ],
        in_specs=[vmem] * 10,
        out_specs=[vmem] * 8,
        scratch_shapes=[
            v(6, *tall),
            v(6, *field),
            v(6, *field),
            v(*field),
            v(*field),
            v(*tall),
            v(*tall),
            v(*field),
            v(*field),
            v(*field),
            v(*field),
            v(2, *wide),
            v(2, *wide),
            v(2, *wide),
            v(*wide),
            v(*wide),
            v(*wide),
            v(*field),
            v(*field),
            v(*field),
            pltpu.VMEM((6, 64, 192), BF16),
            v(3, 64, COLS),
            v(COLS, COLS),
            v(128, COLS),
            v(near, share, COLS),
            v(share, COLS),
            v(far, share, COLS),
            v(share, COLS),
            v(128, COLS),
            v(8, COLS),
            v(near, 8, COLS),
            v(8, COLS),
            v(far, 8, COLS),
            v(12, 2, FEAT, COLS),
            v(12, 2, FEAT, COLS),
            v(12, ROWS, COLS),
            v(12, 2, ROWS, COLS),
            pltpu.SemaphoreType.DMA((12, 4)),
            pltpu.SemaphoreType.DMA((12, 4)),
            pltpu.SemaphoreType.DMA((5, max(near, far))),
            pltpu.SemaphoreType.DMA((5, max(near, far))),
        ],
        compiler_params=pltpu.CompilerParams(
            collective_id=0, has_side_effects=True, vmem_limit_bytes=60 * 1024 * 1024
        ),
    )(
        state.reshape(field),
        mask,
        flux,
        win,
        b_in.reshape(1, HID),
        wmid,
        b_mid.reshape(1, HID),
        wout,
        b_out.reshape(1, FEAT),
        cot.reshape(field),
    )
    shape4 = (4, LEV, ROWS, COLS)
    return (
        out[0].reshape(shape4),
        out[1].reshape(shape4),
        out[2],
        out[3].reshape(HID),
        out[4],
        out[5].reshape(HID),
        out[6],
        out[7].reshape(FEAT),
    )


def solution(mesh):
    block = P(None, None, "lat", "lon")
    return jax.shard_map(
        functools.partial(on_device, mesh.shape["lat"], mesh.shape["lon"]),
        mesh=mesh,
        in_specs=(
            block,
            P(None, "lat", "lon"),
            P("lat", "lon"),
            P(),
            P(),
            P(),
            P(),
            P(),
            P(),
            block,
        ),
        out_specs=(block, block, P(), P(), P(), P(), P(), P()),
        check_vma=False,
    )
```

time: 561 us -> 112 us (0.20); the launches traced: 550 us -> 111 us
  blocking collectives: 148 us -> 0 us
  waiting for transfers between devices: 113 us -> 0 us
  Pallas kernels: 0 us -> 102 us
  local copies, waits for them, and re-layouts: 108 us -> 8.32 us
  other arithmetic: 81 us -> 0 us
  starting transfers between devices: 78.5 us -> 0 us
  matrix products: 17.7 us -> 0 us
    psum x2 -> x0, blocking collectives: 148 us -> none  [the longest x1 76.5 us: on_device(): lax.psum((sum_win, sum_bin, sum_wmid, sum_bmid, sum_wout, sum_bout), ('lo...]
    ppermute x48 -> x0, waiting for transfers between devices: 113 us -> none  [the longest x24 63.4 us: padded_2(): lax.ppermute(tail, axis, [(i, (i + 1) % count) for i in range(count)])]
    pallas_call x0 -> x1, Pallas kernels: none -> 102 us  [on_device(): pl.pallas_call(functools.partial(kernel, lat_count, lon_count), out_shape...]
    ppermute x48 -> x0, starting transfers between devices: 78.5 us -> none  [the longest x24 64.4 us: padded_2(): lax.ppermute(head, axis, [((i + 1) % count, i) for i in range(count)])]
    scatter-add x24 -> x0, local copies, waits for them, and re-layouts: 51.7 us -> none  [the longest x6 25.4 us: fold_back(): interior.at[..., col_count - halo_width:]]
    add x32 -> x0, other arithmetic: 24.4 us -> none  [the longest x6 8.28 us: fold_back(): interior.at[..., col_count - halo_width:]]
    unnamed x286 -> x21, local copies, waits for them, and re-layouts: 32.5 us -> 8.32 us
    mul x40 -> x0, other arithmetic: 22.9 us -> none  [the longest x6 6.19 us: pull_back(): spread = pullback(adjoint)[0] * fence_one]
  transfers between devices with their start and end apart: 48 -> 0, of which waited for: 35 -> 0; matrix products, arithmetic and copies ran while one was open for 7% -> 0% of each run, Pallas kernels for 0% -> 0%
where the time goes in v1:
time: 112 us; the launch traced here: 111 us
  Pallas kernels  102 us (91%)
  local copies, waits for them, and re-layouts  8.32 us (7%)
    pallas_call x1, Pallas kernels, on_device(): pl.pallas_call(functools.partial(kernel, lat_count, lon_count), out_shape...  102 us
    unnamed x21, local copies, waits for them, and re-layouts  8.32 us

profile of v1, /device:TPU:24, one launch (start us, length us, event | category | flops | bytes accessed | tf_op | source)
XLA Modules:
  0.0 111.0 jit_solution(3651222555875184622)
XLA Ops:
  0.6 1.4 %copy.18.wout = f32[64,40]{1,0:T(8,128)} copy(f32[64,40]{0,1:T(8,128)} %param.17) | data formatting | bytes 20480 | tf_op args[7]
  2.1 102.1 %shard_map.161 = (f32[40,16,128]{2,1,0:T(8,128)}, f32[40,16,128]{2,1,0:T(8,128)}, f32[40,64]{1,0:T(8,128)}, f32[1,64]{1,0:T(1,128)}, f32[64,64]{1,0:T(8,128)}, /...) custom-call(f32[40,16,128]{2,1,0:T(8,128)} %bitcast.10, s32[10,16,128]{2,1,0:T(8,128)} %mask.1, f32[16,128]{1,0:T(8,128)} %flux.1, ...), custom_call_target="tpu_custom_call" | custom-call | tf_op jit(solution)/shard_map/pallas_call | solution.py:684
  104.1 1.4 %copy.19 = f32[64,40]{0,1:T(8,128)} copy(f32[64,40]{1,0:T(8,128)} %get-tuple-element.30) | data formatting | bytes 20480
  105.6 0.0 copy-start
  105.6 1.8 %copy.27 = f32[4,10,16,128]{3,2,1,0:T(8,128)} copy(f32[4,10,16,128]{3,2,1,0:T(8,128)} %bitcast.13) | data formatting | bytes 655360
  107.3 0.0 copy-done
  107.3 0.0 copy-start.2
  107.3 0.7 copy.28
  108.1 0.0 copy-done.2
  108.1 0.0 copy-start.5
  108.1 0.0 copy-start.1
  108.1 0.6 copy.29
  108.7 0.0 copy-done.5
  108.7 0.5 copy.30
  109.2 0.0 copy-done.1
  109.2 0.0 copy-start.4
  109.2 0.6 copy.31
  109.9 0.0 copy-done.4
  109.9 0.0 copy-start.3
  109.9 0.5 copy.32
  110.4 0.1 copy-done.3
  110.5 0.5 copy.33
Async XLA Ops:
  105.6 1.8 %copy-start = (f32[40,16,128]{2,1,0:T(8,128)S(1)}, f32[40,16,128]{2,1,0:T(8,128)}, u32[]{:S(2)}) copy-start(f32[40,16,128]{2,1,0:T(8,128)} %get-tuple-element.17) | copy-start | bytes 983044
  107.3 0.7 copy-start.2
  108.1 0.7 copy-start.5
  108.1 1.2 %copy-start.1 = (f32[64,64]{1,0:T(8,128)S(1)}, f32[64,64]{1,0:T(8,128)}, u32[]{:S(2)}) copy-start(f32[64,64]{1,0:T(8,128)} %get-tuple-element.44) | copy-start | bytes 49156
  109.2 0.6 copy-start.4
  109.9 0.7 copy-start.3

commit v2 on v1

--- a/solution.py
+++ b/solution.py
@@ -50,12 +50,7 @@
     cot,
     fin,
     grad,
-    g_win,
-    g_bin,
-    g_wmid,
-    g_bmid,
-    g_wout,
-    g_bout,
+    ag,
     xs,
     ew,
     ns,
@@ -84,7 +79,6 @@
     c1,
     rs2,
     c2,
-    ag,
     f0,
     fr1,
     f1,
@@ -277,6 +271,11 @@
             total = total + slots[d]
         return total
 
+    def levels(body, carry):
+        for l in range(LEV):
+            carry = body(l, carry)
+        return carry
+
     def begin(l, packed):
         wet = depth > l
         for f in range(4):
@@ -287,7 +286,7 @@
         return packed
 
     blank = jnp.zeros((ROWS, COLS), F32)
-    packed = lax.fori_loop(0, LEV, begin, blank)
+    packed = levels(begin, blank)
     col_s[0] = packed
 
     def stage_rows(e, north_ref, south_ref):
@@ -334,7 +333,7 @@
         weight(turned, whole.T[0:64, 0:64])
 
     def prepare():
-        both(wout, HID, FEAT, 3, 2)
+        both(wout, FEAT, HID, 2, 3)
         both(wmid, HID, HID, 4, 1)
         both(win, FEAT, HID, 5, 0)
         square[...] = jnp.zeros((COLS, COLS), F32)
@@ -391,7 +390,7 @@
                 dox[fl] = jnp.where(wet, DT * source[fl], 0.0)
             return carry
 
-        lax.fori_loop(0, LEV, body, 0)
+        levels(body, 0)
         gather(dox, 0, ROWS, dout)
         for c in chunks:
             h = h2[s, :, c]
@@ -451,7 +450,7 @@
         return jnp.where(odd_lane, col_r[e, 1], col_r[e, 0])
 
     def turn(packed, fl):
-        return pltpu.roll(packed, lax.rem(2 * COLS - 1 - 2 * fl, COLS), 1)
+        return pltpu.roll(packed, COLS - 1 - 2 * fl, 1)
 
     def forward(k, forcing):
         start, stage = 3 * (k // 3), k % 3
@@ -500,8 +499,8 @@
                     new = 0.75 * xs[start, fl, 8:24, :] + 0.25 * moved
                 else:
                     given = mx[fl]
-                    if f == 1:
-                        given = given + jnp.where(l == 0, forcing, 0.0)
+                    if f == 1 and l == 0:
+                        given = given + forcing
                     new = (
                         (1.0 / 3.0) * xs[start, fl, 8:24, :]
                         + (2.0 / 3.0) * moved
@@ -514,7 +513,7 @@
                     fin[fl] = new
             return packed, press_x, press_y
 
-        packed, _, _ = lax.fori_loop(0, LEV, body, (blank, blank, blank))
+        packed, _, _ = levels(body, (blank, blank, blank))
         if k < 5:
             col_s[k + 1] = packed
             stage_rows(k + 1, xs.at[k + 1], xs.at[k + 1])
@@ -571,7 +570,7 @@
                 acc[fl] = own
             return packed, sum_u, sum_v
 
-        packed, _, _ = lax.fori_loop(0, LEV, body, (blank, blank, blank))
+        packed, _, _ = levels(body, (blank, blank, blank))
         col_s[6 + n] = packed
         stage_rows(6 + n, mn, pn)
         launch(6 + n)
@@ -601,7 +600,7 @@
                         lam[fl] = new
             return carry
 
-        lax.fori_loop(0, LEV, body, 0)
+        levels(body, 0)
 
     prepare()
     layer_one(0)
@@ -660,15 +659,19 @@
     for stage in range(4):
         fan_drain(stage)
     fan_arrive(4)
-    top = ag[0:64]
-    g_wmid[...] = top[:, 0:HID]
-    g_wout[...] = pltpu.roll(top, 64, 1)[:, 0:FEAT]
-    g_win[...] = ag[64:104][:, 0:HID]
+    fan_drain(4)
+
+
+def unpack(fin, grad, ag, o_fin, o_grad, g_win, g_bin, g_wmid, g_bmid, g_wout, g_bout):
+    o_fin[...] = fin[...]
+    o_grad[...] = grad[...]
+    g_wmid[...] = ag[0:64, 0:HID]
+    g_wout[...] = pltpu.roll(ag[0:COLS], 64, 1).T[0:FEAT, 0:HID]
+    g_win[...] = ag[64:104, 0:HID]
     sums = ag[104:112]
     g_bin[...] = sums[0:1, 0:HID]
     g_bmid[...] = sums[1:2, 0:HID]
     g_bout[...] = sums[2:3, 0:FEAT]
-    fan_drain(4)
 
 
 def on_device(lat_count, lon_count, state, mask, flux, win, b_in, wmid, b_mid, wout, b_out, cot):
@@ -683,21 +686,9 @@
     wide = (64, CELLS)
     out = pl.pallas_call(
         functools.partial(kernel, lat_count, lon_count),
-        out_shape=[
-            jax.ShapeDtypeStruct(shape, F32)
-            for shape in (
-                field,
-                field,
-                (FEAT, HID),
-                (1, HID),
-                (HID, HID),
-                (1, HID),
-                (HID, FEAT),
-                (1, FEAT),
-            )
-        ],
+        out_shape=[jax.ShapeDtypeStruct(shape, F32) for shape in (field, field, (128, COLS))],
         in_specs=[vmem] * 10,
-        out_specs=[vmem] * 8,
+        out_specs=[vmem] * 3,
         scratch_shapes=[
             v(6, *tall),
             v(6, *field),
@@ -727,7 +718,6 @@
             v(share, COLS),
             v(far, share, COLS),
             v(share, COLS),
-            v(128, COLS),
             v(8, COLS),
             v(near, 8, COLS),
             v(8, COLS),
@@ -752,10 +742,28 @@
         b_in.reshape(1, HID),
         wmid,
         b_mid.reshape(1, HID),
-        wout,
+        wout.T,
         b_out.reshape(1, FEAT),
         cot.reshape(field),
     )
+    out = pl.pallas_call(
+        unpack,
+        out_shape=[
+            jax.ShapeDtypeStruct(shape, F32)
+            for shape in (
+                field,
+                field,
+                (FEAT, HID),
+                (1, HID),
+                (HID, HID),
+                (1, HID),
+                (FEAT, HID),
+                (1, FEAT),
+            )
+        ],
+        in_specs=[vmem] * 3,
+        out_specs=[vmem] * 8,
+    )(*out)
     shape4 = (4, LEV, ROWS, COLS)
     return (
         out[0].reshape(shape4),
@@ -764,7 +772,7 @@
         out[3].reshape(HID),
         out[4],
         out[5].reshape(HID),
-        out[6],
+        out[6].T,
         out[7].reshape(FEAT),
     )
 

time: 112 us -> 86.4 us (0.77)
  Pallas kernels: 102 us -> 84.9 us
  local copies, waits for them, and re-layouts: 8.32 us -> 0 us
    pallas_call x1, Pallas kernels: 102 us -> 82.9 us  [on_device(): pl.pallas_call(functools.partial(kernel, lat_count, lon_count), out_shape...]
    unnamed x21 -> x0, local copies, waits for them, and re-layouts: 8.32 us -> none
    pallas_call x0 -> x1, Pallas kernels: none -> 2 us  [on_device(): pl.pallas_call(unpack, out_shape=[jax.ShapeDtypeStruct(shape, F32) for sh...]
where the time goes in v2:
time: 86.4 us; the launch traced here: 85.5 us
  Pallas kernels  84.9 us (98%)
    pallas_call x1, Pallas kernels, on_device(): pl.pallas_call(functools.partial(kernel, lat_count, lon_count), out_shape...  82.9 us
    pallas_call x1, Pallas kernels, on_device(): pl.pallas_call(unpack, out_shape=[jax.ShapeDtypeStruct(shape, F32) for sh...  2 us

profile of v2, /device:TPU:24, one launch (start us, length us, event | category | flops | bytes accessed | tf_op | source)
XLA Modules:
  0.0 85.5 jit_solution(7156381876196559198)
XLA Ops:
  0.6 82.9 %shard_map.161 = (f32[40,16,128]{2,1,0:T(8,128)}, f32[40,16,128]{2,1,0:T(8,128)}, f32[128,128]{1,0:T(8,128)}) custom-call(f32[40,16,128]{2,1,0:T(8,128)} %bitcast.12, s32[10,16,128]{2,1,0:T(8,128)} %mask.1, f32[16,128]{1,0:T(8,128)} %flux.1, f32[40,64]{1,0:T(8,128)} %win.1, f32[1,64]{1,0:T(1,128)} %bitcast.15, f32[64,64]{1,0:T(8,128)} %wmid.1, ...), custom_call_target="tpu_custom_call" | custom-call | tf_op jit(solution)/shard_map/pallas_call | solution.py:687
  83.5 2.0 %shard_map.162 = (f32[40,16,128]{2,1,0:T(8,128)}, f32[40,16,128]{2,1,0:T(8,128)}, f32[40,64]{1,0:T(8,128)}, f32[1,64]{1,0:T(1,128)}, f32[64,64]{1,0:T(8,128)}, /...) custom-call(f32[40,16,128]{2,1,0:T(8,128)} %get-tuple-element.19.fin, f32[40,16,128]{2,1,0:T(8,128)} %get-tuple-element.20.grad, ...), custom_call_target="tpu_custom_call" | custom-call | tf_op jit(solution)/shard_map/pallas_call | solution.py:749

commit v3 on v2

--- a/solution.py
+++ b/solution.py
@@ -18,6 +18,7 @@
 ROWS = 16
 COLS = 128
 CELLS = ROWS * COLS
+TALL = 24
 PAD = 32
 
 LAT_LIMIT = 1.2
@@ -52,6 +53,7 @@
     grad,
     ag,
     xs,
+    ewsum,
     ew,
     ns,
     pe,
@@ -87,8 +89,20 @@
     row_r,
     col_s,
     col_r,
+    xh,
+    st,
+    sd,
+    dh,
+    wrow_s,
+    wrow_r,
+    wst_s,
+    wst_r,
+    wc_s,
+    wc_r,
     h_send,
     h_recv,
+    w_send,
+    w_recv,
     a_send,
     a_recv,
 ):
@@ -102,22 +116,30 @@
     near = lon_count // halves
     far = lat_count * halves
     share = 128 // near
-    half = lon // near
+    half = lax.div(lon, jnp.int32(near))
     spot = lon - half * near
-    other = lat * halves + half
+
+    def wrap(at, count):
+        return at - count * lax.div(at, jnp.int32(count))
+
+    near_spots = [wrap(spot + d, near) for d in range(near)]
+    far_lats = [wrap(lat + d, lat_count) for d in range(lat_count)]
+    far_lons = [half * near + spot, (1 - half) * near + spot]
 
     def along(d):
-        return {"lon": half * near + lax.rem(spot + d, near), "lat": lat}
+        return {"lon": half * near + near_spots[d], "lat": lat}
 
     def across(d):
-        to = lax.rem(other + d, far)
-        to_lat = to // halves
-        return {"lon": (to - to_lat * halves) * near + spot, "lat": to_lat}
+        return {"lon": far_lons[d % halves], "lat": far_lats[d // halves]}
 
     north_id = {"lon": lon, "lat": lat + 1}
     south_id = {"lon": lon, "lat": lat - 1}
     east_id = {"lon": east, "lat": lat}
     west_id = {"lon": west, "lat": lat}
+    ne_id = {"lon": east, "lat": lat + 1}
+    nw_id = {"lon": west, "lat": lat + 1}
+    se_id = {"lon": east, "lat": lat - 1}
+    sw_id = {"lon": west, "lat": lat - 1}
 
     barrier = pltpu.get_barrier_semaphore()
 
@@ -130,23 +152,28 @@
     @pl.when(has_n)
     def _():
         greet(north_id)
+        greet(ne_id)
+        greet(nw_id)
 
     @pl.when(has_s)
     def _():
         greet(south_id)
+        greet(se_id)
+        greet(sw_id)
 
     for d in range(1, near):
         greet(along(d))
     for d in range(1, far):
         greet(across(d))
 
-    lane = lax.broadcasted_iota(jnp.int32, (ROWS, COLS), 1)
-    row = lax.broadcasted_iota(jnp.int32, (ROWS, COLS), 0)
-    first_lane = lane == 0
-    last_lane = lane == COLS - 1
+    lane24 = lax.broadcasted_iota(jnp.int32, (TALL, COLS), 1)
+    row24 = lax.broadcasted_iota(jnp.int32, (TALL, COLS), 0)
+    lane = lane24[0:ROWS]
+    row = row24[0:ROWS]
     odd_lane = lax.rem(lane, 2) == 1
     low_lane = lane < 64
-    grow = (row + lat * ROWS).astype(F32)
+    place = row24 + jnp.where(row24 < 16, 0, jnp.where(row24 < 20, -19, -5))
+    grow = jnp.clip(place + lat * ROWS, 0, lat_count * ROWS - 1).astype(F32)
     phi = LAT_LIMIT * (2.0 * (grow + 0.5) / (lat_count * ROWS) - 1.0)
     sq = phi * phi
     cosine = jnp.ones_like(phi)
@@ -154,13 +181,17 @@
     for n in range(8, 0, -1):
         cosine = 1.0 - cosine * sq * (1.0 / ((2 * n - 1) * (2 * n)))
         sine = 1.0 - sine * sq * (1.0 / ((2 * n) * (2 * n + 1)))
-    inv_cos = 1.0 / cosine
-    cor = sine * phi
-    hm = 0.5 * inv_cos
-    cc = inv_cos * inv_cos
+    inv24 = 1.0 / cosine
+    cor24 = sine * phi
+    hm24 = 0.5 * inv24
+    cc24 = inv24 * inv24
+    cor, hm, cc = cor24[0:ROWS], hm24[0:ROWS], cc24[0:ROWS]
     depth = mask[0]
     for l in range(1, LEV):
         depth = depth + mask[l]
+    depth_own = depth.astype(F32)
+    group = lax.div(lane24, jnp.int32(12))
+    slot = lane24 - 12 * group
 
     def hcopy(e, d):
         if d == 0:
@@ -216,6 +247,130 @@
         hcopy(e, 2).wait_send()
         hcopy(e, 3).wait_send()
 
+    def wcopy(e, d):
+        count = 48 if e == 0 else FEAT
+        fields = 5 if e == 0 else 4
+        if d < 2:
+            src = wrow_s.at[e, d, :, 0:count]
+            dst = wrow_r.at[e, d, :, 0:count]
+            to = (north_id, south_id)[d]
+        elif d < 4:
+            src = wst_s.at[e, 0:fields]
+            dst = wst_r.at[e, d - 2, 0:fields]
+            to = (east_id, west_id)[d - 2]
+        else:
+            src = wc_s.at[e, (d - 4) // 3]
+            dst = wc_r.at[e, d - 4]
+            to = (north_id, ne_id, nw_id, south_id, se_id, sw_id)[d - 4]
+        return pltpu.make_async_remote_copy(
+            src_ref=src,
+            dst_ref=dst,
+            send_sem=w_send.at[e, d],
+            recv_sem=w_recv.at[e, d],
+            device_id=to,
+            device_id_type=MESH,
+        )
+
+    north_ones = (0, 4, 5, 6)
+    south_ones = (1, 7, 8, 9)
+
+    def wide_launch(e):
+        @pl.when(has_n)
+        def _():
+            for d in north_ones:
+                wcopy(e, d).start()
+
+        @pl.when(has_s)
+        def _():
+            for d in south_ones:
+                wcopy(e, d).start()
+
+        wcopy(e, 2).start()
+        wcopy(e, 3).start()
+
+    def wide_arrive(e):
+        @pl.when(has_s)
+        def _():
+            for d in north_ones:
+                wcopy(e, d).wait_recv()
+
+        @pl.when(has_n)
+        def _():
+            for d in south_ones:
+                wcopy(e, d).wait_recv()
+
+        wcopy(e, 2).wait_recv()
+        wcopy(e, 3).wait_recv()
+
+    def wide_drain(e):
+        @pl.when(has_n)
+        def _():
+            for d in north_ones:
+                wcopy(e, d).wait_send()
+
+        @pl.when(has_s)
+        def _():
+            for d in south_ones:
+                wcopy(e, d).wait_send()
+
+        wcopy(e, 2).wait_send()
+        wcopy(e, 3).wait_send()
+
+    def strip_pack(strip, value, l):
+        low = pltpu.roll(value, 12 * l + 3, 1)
+        high = pltpu.roll(value, (12 * l + 9) % COLS, 1)
+        here = (lane >= 12 * l + 3) & (lane < 12 * l + 6)
+        there = (lane >= 12 * l + 6) & (lane < 12 * l + 9)
+        return jnp.where(here, low, jnp.where(there, high, strip))
+
+    def wide_stage(e, strips):
+        k = 3 * e
+        for j in range(3):
+            wrow_s[e, 0, j, 0:FEAT] = take_rows(xs.at[k], 21 + j, PAD)
+            wrow_s[e, 1, j, 0:FEAT] = take_rows(xs.at[k], 8 + j, PAD)
+            if e == 0:
+                wrow_s[e, 0, j, 40:48] = jnp.broadcast_to(depth_own[13 + j : 14 + j], (8, COLS))
+                wrow_s[e, 1, j, 40:48] = jnp.broadcast_to(depth_own[j : j + 1], (8, COLS))
+        if e == 1:
+            wc_s[e] = jnp.zeros((2, 16, COLS), F32)
+        for f, strip in enumerate(strips):
+            wst_s[e, f] = strip
+            wc_s[e, 0, 3 * f : 3 * f + 3] = strip[13:16]
+            wc_s[e, 1, 3 * f : 3 * f + 3] = strip[0:3]
+
+    def pick(from_west, own, from_east, slots):
+        return jnp.where(
+            slots < 3,
+            pltpu.roll(from_west, COLS - 6, 1),
+            jnp.where(slots >= 9, pltpu.roll(from_east, 6, 1), own),
+        )
+
+    def wide_unpack(e):
+        k = 3 * e
+        put_rows(xs.at[k], 7, PAD, wrow_r[e, 0, 2, 0:FEAT])
+        put_rows(xs.at[k], 24, PAD, wrow_r[e, 1, 0, 0:FEAT])
+        for j in range(3):
+            put_rows(xh.at[k], j, 8, wrow_r[e, 0, j, 0:FEAT])
+            put_rows(xh.at[k], 5 + j, 8, wrow_r[e, 1, j, 0:FEAT])
+        put_rows(xh.at[k], 3, 8, take_rows(xs.at[k], 8, PAD))
+        put_rows(xh.at[k], 4, 8, take_rows(xs.at[k], 23, PAD))
+        slots = slot[0:ROWS]
+        below = pick(wc_r[e, 1], wc_r[e, 0], wc_r[e, 2], slots)
+        above = pick(wc_r[e, 4], wc_r[e, 3], wc_r[e, 5], slots)
+        for f in range(5 if e == 0 else 4):
+            own = pick(wst_r[e, 0, f], wst_s[e, f], wst_r[e, 1, f], slots)
+            to = st.at[k, f] if f < 4 else sd
+            to[0:16, :] = own
+            to[16:19, :] = below[3 * f : 3 * f + 3]
+            to[19:20, :] = own[0:1]
+            to[20:21, :] = own[15:16]
+            to[21:24, :] = above[3 * f : 3 * f + 3]
+        if e == 0:
+            dh[...] = jnp.zeros((8, COLS), F32)
+            for j in range(3):
+                dh[j : j + 1] = wrow_r[e, 0, j, 40:41]
+                dh[5 + j : 6 + j] = wrow_r[e, 1, j, 40:41]
+
     def take_rows(ref, r, count):
         return ref.reshape(FEAT * count, COLS)[pl.ds(r, FEAT, stride=count), :]
 
@@ -248,7 +403,7 @@
         if stage == 1:
             return fan(stage, d, f1, fr2.at[d], across(d))
         if stage == 2:
-            return fan(stage, d, gb.at[part(lax.rem(spot + d, near))], rs1.at[d], along(d))
+            return fan(stage, d, gb.at[part(near_spots[d])], rs1.at[d], along(d))
         if stage == 3:
             return fan(stage, d, c1, rs2.at[d], across(d))
         return fan(stage, d, c2, ag.at[part(spot)], along(d))
@@ -276,24 +431,23 @@
             carry = body(l, carry)
         return carry
 
-    def begin(l, packed):
+    blank = jnp.zeros((ROWS, COLS), F32)
+    strips = [blank] * 5
+    for l in range(LEV):
         wet = depth > l
         for f in range(4):
             fl = f * LEV + l
             x = jnp.where(wet, state[fl], 0.0)
             xs[0, fl, 8:24, :] = x
-            packed = pack(packed, x, fl)
-        return packed
-
-    blank = jnp.zeros((ROWS, COLS), F32)
-    packed = levels(begin, blank)
-    col_s[0] = packed
+            strips[f] = strip_pack(strips[f], x, l)
+        strips[4] = strip_pack(strips[4], depth_own, l)
+    wc_s[0] = jnp.zeros((2, 16, COLS), F32)
+    wide_stage(0, strips)
 
     def stage_rows(e, north_ref, south_ref):
         row_s[e, 0] = take_rows(north_ref, 23, PAD)
         row_s[e, 1] = take_rows(south_ref, 8, PAD)
 
-    stage_rows(0, xs.at[0], xs.at[0])
     wet_top = depth > 0
     part_flux = jnp.sum(jnp.where(wet_top, flux[...], 0.0), axis=0, keepdims=True)
     part_count = jnp.sum(jnp.where(wet_top, 1.0, 0.0), axis=0, keepdims=True)
@@ -304,20 +458,28 @@
         jnp.where(row8 == 1, jnp.broadcast_to(part_count, (8, COLS)), 0.0),
     )
 
-    meet = near + far + has_n.astype(jnp.int32) + has_s.astype(jnp.int32)
+    meet = near + far + 3 * has_n.astype(jnp.int32) + 3 * has_s.astype(jnp.int32)
     pl.semaphore_wait(barrier, meet)
-    launch(0)
+    wide_launch(0)
     fan_start(0)
 
     @pl.when(jnp.logical_not(has_s))
     def _():
-        for e in range(12):
+        for e in range(6):
             row_r[e, 0] = jnp.zeros((FEAT, COLS), F32)
+        for e in range(2):
+            wrow_r[e, 0] = jnp.zeros((3, 48, COLS), F32)
+            for d in range(3):
+                wc_r[e, d] = jnp.zeros((16, COLS), F32)
 
     @pl.when(jnp.logical_not(has_n))
     def _():
-        for e in range(12):
+        for e in range(6):
             row_r[e, 1] = jnp.zeros((FEAT, COLS), F32)
+        for e in range(2):
+            wrow_r[e, 1] = jnp.zeros((3, 48, COLS), F32)
+            for d in range(3, 6):
+                wc_r[e, d] = jnp.zeros((16, COLS), F32)
 
     def weight(at, value):
         hi, lo = split(value)
@@ -347,6 +509,8 @@
             zc[s, FEAT:64, :] = jnp.zeros((64 - FEAT, CELLS), F32)
         dout[FEAT:64, :] = jnp.zeros((64 - FEAT, CELLS), F32)
         gb[112:128] = jnp.zeros((16, COLS), F32)
+        put_rows(mn, 7, PAD, jnp.zeros((FEAT, COLS), F32))
+        put_rows(pn, 24, PAD, jnp.zeros((FEAT, COLS), F32))
 
     def product(at, x):
         hi, lo = split(x)
@@ -441,83 +605,161 @@
             gb[64:104] = low
             gb[104:112] = sums
 
-    def sides(turned, q_west, q_east):
-        w_side = pltpu.roll(jnp.where(last_lane, turned, q_west), 1, 1)
-        e_side = pltpu.roll(jnp.where(first_lane, turned, q_east), COLS - 1, 1)
-        return w_side, e_side
-
-    def halo(e):
-        return jnp.where(odd_lane, col_r[e, 1], col_r[e, 0])
-
-    def turn(packed, fl):
-        return pltpu.roll(packed, COLS - 1 - 2 * fl, 1)
+    first_lane = lane == 0
+    last_lane = lane == COLS - 1
+
+    def add_rows(ref, r, value):
+        view = ref.reshape(FEAT * ROWS, COLS)
+        view[pl.ds(r, FEAT, stride=ROWS), :] = view[pl.ds(r, FEAT, stride=ROWS), :] + value
+
+    def tendency(f, q, d_x, d_y, sum_x, sum_y, u, v, p_x, p_y, coef):
+        c_hm, c_cc, c_cor = coef
+        mix = MIX[f]
+        change = (
+            (mix * c_cc) * (sum_x - 2.0 * q)
+            + mix * (sum_y - 2.0 * q)
+            - ((u * c_hm) * d_x + (v * 0.5) * d_y)
+        )
+        if f == 2:
+            change = change + (c_cor * v - p_x * c_hm)
+        if f == 3:
+            change = change - (c_cor * u + p_y * 0.5)
+        return DT * change
+
+    def rise(own, edge):
+        own_n = jnp.where(
+            row == 15, jnp.broadcast_to(edge[5:6], (ROWS, COLS)), pltpu.roll(own, 15, 0)
+        )
+        own_s = jnp.where(
+            row == 0, jnp.broadcast_to(edge[2:3], (ROWS, COLS)), pltpu.roll(own, 1, 0)
+        )
+        return (
+            jnp.concatenate([own_n, pltpu.roll(edge, 7, 0)], axis=0),
+            jnp.concatenate([own_s, pltpu.roll(edge, 1, 0)], axis=0),
+        )
+
+    def mend(edge, own):
+        rows8 = row24[0:8]
+        first = jnp.broadcast_to(own[0:1], (8, COLS))
+        last = jnp.broadcast_to(own[15:16], (8, COLS))
+        return jnp.where(rows8 == 3, first, jnp.where(rows8 == 4, last, edge))
+
+    def strip_section(k):
+        start, stage = 3 * (k // 3), k % 3
+        wet = (group.astype(F32) < sd[...]) & (lane24 < 12 * LEV)
+        q = [st[k, f] for f in range(4)]
+        d_x, d_y, sum_x, sum_y = [], [], [], []
+        for f in range(4):
+            east_q = pltpu.roll(q[f], COLS - 1, 1)
+            west_q = pltpu.roll(q[f], 1, 1)
+            north_q, south_q = rise(q[f][0:16], q[f][16:24])
+            d_x.append(east_q - west_q)
+            d_y.append(north_q - south_q)
+            sum_x.append(east_q + west_q)
+            sum_y.append(north_q + south_q)
+
+        def down(slope):
+            total = GAIN_T * slope[0] + GAIN_S * slope[1]
+            for hop in (12, 24, 48, 96):
+                total = total + jnp.where(lane24 >= hop, pltpu.roll(total, hop, 1), 0.0)
+            return total
+
+        p_x, p_y = down(d_x), down(d_y)
+        for f in range(4):
+            change = tendency(
+                f, q[f], d_x[f], d_y[f], sum_x[f], sum_y[f], q[2], q[3], p_x, p_y,
+                (hm24, cc24, cor24),
+            )
+            moved = q[f] + jnp.where(wet, change, 0.0)
+            new = moved if stage == 0 else 0.75 * st[start, f] + 0.25 * moved
+            st[k + 1, f, 0:16, :] = new[0:16]
+            st[k + 1, f, 16:24, :] = mend(new[16:24], new[0:16])
 
     def forward(k, forcing):
-        start, stage = 3 * (k // 3), k % 3
-        arrive(k)
-        put_rows(xs.at[k], 7, PAD, row_r[k, 0])
-        put_rows(xs.at[k], 24, PAD, row_r[k, 1])
-        received = halo(k)
-
-        def body(l, carry):
-            packed, press_x, press_y = carry
-            wet = depth > l
-            u = xs[k, 2 * LEV + l, 8:24, :]
-            v = xs[k, 3 * LEV + l, 8:24, :]
-            uh = u * hm
-            vh = v * 0.5
+        e, start, stage = k // 3, 3 * (k // 3), k % 3
+        if stage == 0:
+            wide_arrive(e)
+            wide_unpack(e)
+        tall = TALL if stage < 2 else ROWS
+        lanes = lane24[0:tall]
+        first, last = lanes == 0, lanes == COLS - 1
+        coef = (hm24[0:tall], cc24[0:tall], cor24[0:tall])
+        if tall == TALL:
+            deep = jnp.concatenate([depth_own, dh[...]], axis=0)
+        else:
+            deep = depth_own
+        rows8 = row24[0:8]
+        strips = [blank] * 4
+        edges = [st[k, f, 0:tall, :] for f in range(4)]
+        press_x = press_y = jnp.zeros((tall, COLS), F32)
+
+        def value(at, fl):
+            own = xs[at, fl, 8:24, :]
+            return jnp.concatenate([own, xh[at, fl]], axis=0) if tall == TALL else own
+
+        for l in range(LEV):
             for f in range(4):
                 fl = f * LEV + l
-                q = xs[k, fl, 8:24, :]
+                q = value(k, fl)
+                from_w = pltpu.roll(edges[f], (2 * COLS - 2 - 12 * l) % COLS, 1)
+                from_e = pltpu.roll(edges[f], (2 * COLS - 10 - 12 * l) % COLS, 1)
+                w_side = jnp.where(first, from_w, pltpu.roll(q, 1, 1))
+                e_side = jnp.where(last, from_e, pltpu.roll(q, COLS - 1, 1))
+                ew[k, fl, 0:tall] = e_side - w_side
+                ewsum[fl, 0:tall] = e_side + w_side
+
+        for l in range(LEV):
+            wet = deep > float(l)
+            u = value(k, 2 * LEV + l)
+            v = value(k, 3 * LEV + l)
+            for f in range(4):
+                fl = f * LEV + l
+                q = value(k, fl)
                 north = xs[k, fl, 9:25, :]
                 south = xs[k, fl, 7:23, :]
-                w_side, e_side = sides(turn(received, fl), q, q)
-                d_x = e_side - w_side
+                if tall == TALL:
+                    edge = xh[k, fl]
+                    north = jnp.concatenate([north, pltpu.roll(edge, 7, 0)], axis=0)
+                    south = jnp.concatenate([south, pltpu.roll(edge, 1, 0)], axis=0)
+                d_x = ew[k, fl, 0:tall]
                 d_y = north - south
-                ew[k, fl] = d_x
-                ns[k, fl] = d_y
-                mix = MIX[f]
-                change = (
-                    (mix * cc) * (e_side + w_side - 2.0 * q)
-                    + mix * (north + south - 2.0 * q)
-                    - (uh * d_x + vh * d_y)
+                ns[k, fl] = d_y[0:ROWS]
+                if f < 2:
+                    press_x = press_x + (GAIN_T, GAIN_S)[f] * d_x
+                    press_y = press_y + (GAIN_T, GAIN_S)[f] * d_y
+                change = tendency(
+                    f, q, d_x, d_y, ewsum[fl, 0:tall], north + south, u, v, press_x, press_y, coef
                 )
-                if f == 0:
-                    press_x = press_x + GAIN_T * d_x
-                    press_y = press_y + GAIN_T * d_y
-                if f == 1:
-                    press_x = press_x + GAIN_S * d_x
-                    press_y = press_y + GAIN_S * d_y
-                if f == 2:
-                    change = change + (cor * v - press_x * hm)
-                if f == 3:
-                    change = change - (cor * u + press_y * 0.5)
-                moved = q + jnp.where(wet, DT * change, 0.0)
+                moved = q + jnp.where(wet, change, 0.0)
                 if stage == 0:
                     new = moved
                 elif stage == 1:
-                    new = 0.75 * xs[start, fl, 8:24, :] + 0.25 * moved
+                    new = 0.75 * value(start, fl) + 0.25 * moved
                 else:
                     given = mx[fl]
                     if f == 1 and l == 0:
                         given = given + forcing
                     new = (
-                        (1.0 / 3.0) * xs[start, fl, 8:24, :]
+                        (1.0 / 3.0) * value(start, fl)
                         + (2.0 / 3.0) * moved
                         + jnp.where(wet, DT * given, 0.0)
                     )
-                if k < 5:
+                if stage < 2:
+                    own, edge = new[0:ROWS], new[ROWS:TALL]
+                    xs[k + 1, fl, 8:24, :] = own
+                    xs[k + 1, fl, 7:8, :] = edge[2:3]
+                    xs[k + 1, fl, 24:25, :] = edge[5:6]
+                    xh[k + 1, fl] = mend(edge, own)
+                elif k == 2:
                     xs[k + 1, fl, 8:24, :] = new
-                    packed = pack(packed, new, fl)
+                    strips[f] = strip_pack(strips[f], new, l)
                 else:
                     fin[fl] = new
-            return packed, press_x, press_y
-
-        packed, _, _ = levels(body, (blank, blank, blank))
-        if k < 5:
-            col_s[k + 1] = packed
-            stage_rows(k + 1, xs.at[k + 1], xs.at[k + 1])
-            launch(k + 1)
+        if stage < 2:
+            strip_section(k)
+        elif k == 2:
+            wide_stage(1, strips)
+            wide_launch(1)
 
     def give(n, source):
         k, stage = 5 - n, (5 - n) % 3
@@ -536,8 +778,6 @@
             vh = v * 0.5
             push_x = hm * sum_u
             push_y = 0.5 * sum_v
-            to_u = cor * g[3]
-            to_v = cor * g[2]
             for f in range(4):
                 fl = f * LEV + l
                 mix = MIX[f]
@@ -558,8 +798,25 @@
                 pn[fl, 8:24, :] = flat + b
                 mn[fl, 8:24, :] = flat - b
                 packed = pack(packed, jnp.where(low_lane, plus, minus), fl)
-                to_u = to_u + g[f] * (hm * ew[k, fl])
-                to_v = to_v - g[f] * (0.5 * ns[k, fl])
+            return packed, sum_u, sum_v
+
+        packed, _, _ = levels(body, (blank, blank, blank))
+        col_s[n] = packed
+        stage_rows(n, mn, pn)
+        launch(n)
+
+    def keep(n, source):
+        k, stage = 5 - n, (5 - n) % 3
+        scale = (1.0, 0.25, 2.0 / 3.0)[stage]
+        for l in range(LEV):
+            wet = depth > l
+            g = [jnp.where(wet, (DT * scale) * source[f * LEV + l], 0.0) for f in range(4)]
+            along_x = along_y = blank
+            for f in range(4):
+                along_x = along_x + g[f] * ew[k, f * LEV + l, 0:ROWS]
+                along_y = along_y + g[f] * ns[k, f * LEV + l]
+            to_u = cor * g[3] + hm * along_x
+            to_v = cor * g[2] - 0.5 * along_y
             for f in range(4):
                 fl = f * LEV + l
                 own = -2.0 * (MIX[f] * cc + MIX[f]) * g[f]
@@ -567,27 +824,25 @@
                     own = own - to_u
                 if f == 3:
                     own = own + to_v
-                acc[fl] = own
-            return packed, sum_u, sum_v
-
-        packed, _, _ = levels(body, (blank, blank, blank))
-        col_s[6 + n] = packed
-        stage_rows(6 + n, mn, pn)
-        launch(6 + n)
+                w_side = jnp.where(first_lane, 0.0, pltpu.roll(mw[fl], 1, 1))
+                e_side = jnp.where(last_lane, 0.0, pltpu.roll(pe[fl], COLS - 1, 1))
+                acc[fl] = own + w_side + e_side + pn[fl, 9:25, :] + mn[fl, 7:23, :]
 
     def take(n, source):
         stage = (5 - n) % 3
-        e = 6 + n
+        e = n
         arrive(e)
-        put_rows(mn, 7, PAD, row_r[e, 0])
-        put_rows(pn, 24, PAD, row_r[e, 1])
-        received = halo(e)
+        add_rows(acc, 0, row_r[e, 0])
+        add_rows(acc, 15, row_r[e, 1])
+        received = jnp.where(
+            odd_lane, pltpu.roll(col_r[e, 0], 1, 1), pltpu.roll(col_r[e, 1], COLS - 1, 1)
+        )
 
         def body(l, carry):
             for f in range(4):
                 fl = f * LEV + l
-                w_side, e_side = sides(turn(received, fl), mw[fl], pe[fl])
-                got = acc[fl] + w_side + e_side + pn[fl, 9:25, :] + mn[fl, 7:23, :]
+                turned = pltpu.roll(received, COLS - 1 - 2 * fl, 1)
+                got = acc[fl] + jnp.where(first_lane | last_lane, turned, 0.0)
                 if stage == 2:
                     t2[fl] = (2.0 / 3.0) * source[fl] + got
                 elif stage == 1:
@@ -604,13 +859,13 @@
 
     prepare()
     layer_one(0)
-    forward(0, None)
+    layer_two(0)
+    layer_three(0)
     fan_arrive(0)
     f1[...] = slot_sum(0, f0[...], fr1)
     fan_start(1)
-    layer_two(0)
+    forward(0, None)
     forward(1, None)
-    layer_three(0)
     fan_arrive(1)
     totals = slot_sum(1, f1[...], fr2)
     flux_sum = jnp.sum(totals[0:1, :], axis=1, keepdims=True)
@@ -619,32 +874,38 @@
     forcing = -FRESHWATER * (flux[...] - mean)
     forward(2, forcing)
     layer_one(1)
+    layer_two(1)
+    layer_three(1)
+    back_out(1, cot)
+    back_mid(1)
+    back_in(1)
     forward(3, None)
-    layer_two(1)
     forward(4, None)
-    layer_three(1)
+
+    give(0, cot)
     forward(5, forcing)
-
-    give(0, cot)
-    back_out(1, cot)
+    keep(0, cot)
     take(0, cot)
     give(1, t2)
-    back_mid(1)
-    back_in(1)
+    keep(1, t2)
+    weight_grads(1, False)
     take(1, cot)
     give(2, t1)
-    weight_grads(1, False)
+    keep(2, t1)
     take(2, cot)
     give(3, lam)
+    keep(3, lam)
     back_out(0, lam)
     back_mid(0)
     take(3, lam)
     give(4, t2)
+    keep(4, t2)
     weight_grads(0, True)
     fan_start(2)
     back_in(0)
     take(4, lam)
     give(5, t1)
+    keep(5, t1)
     fan_arrive(2)
     c1[...] = slot_sum(2, gb[part(spot)], rs1)
     fan_start(3)
@@ -654,8 +915,10 @@
     c2[...] = slot_sum(3, c1[...], rs2) * scale
     ag[part(spot)] = c2[...]
     fan_start(4)
-    for e in range(12):
+    for e in range(6):
         drain(e)
+    for e in range(2):
+        wide_drain(e)
     for stage in range(4):
         fan_drain(stage)
     fan_arrive(4)
@@ -691,7 +954,8 @@
         out_specs=[vmem] * 3,
         scratch_shapes=[
             v(6, *tall),
-            v(6, *field),
+            v(FEAT, TALL, COLS),
+            v(6, FEAT, TALL, COLS),
             v(6, *field),
             v(*field),
             v(*field),
@@ -722,12 +986,24 @@
             v(near, 8, COLS),
             v(8, COLS),
             v(far, 8, COLS),
-            v(12, 2, FEAT, COLS),
-            v(12, 2, FEAT, COLS),
-            v(12, ROWS, COLS),
-            v(12, 2, ROWS, COLS),
-            pltpu.SemaphoreType.DMA((12, 4)),
-            pltpu.SemaphoreType.DMA((12, 4)),
+            v(6, 2, FEAT, COLS),
+            v(6, 2, FEAT, COLS),
+            v(6, ROWS, COLS),
+            v(6, 2, ROWS, COLS),
+            v(6, FEAT, 8, COLS),
+            v(6, 4, TALL, COLS),
+            v(TALL, COLS),
+            v(8, COLS),
+            v(2, 2, 3, 48, COLS),
+            v(2, 2, 3, 48, COLS),
+            v(2, 5, ROWS, COLS),
+            v(2, 2, 5, ROWS, COLS),
+            v(2, 2, 16, COLS),
+            v(2, 6, 16, COLS),
+            pltpu.SemaphoreType.DMA((6, 4)),
+            pltpu.SemaphoreType.DMA((6, 4)),
+            pltpu.SemaphoreType.DMA((2, 10)),
+            pltpu.SemaphoreType.DMA((2, 10)),
             pltpu.SemaphoreType.DMA((5, max(near, far))),
             pltpu.SemaphoreType.DMA((5, max(near, far))),
         ],

time: 86.4 us -> 70.9 us (0.82)
  Pallas kernels: 84.9 us -> 69.2 us
    pallas_call x1, Pallas kernels: 82.9 us -> 67.2 us  [on_device(): pl.pallas_call(functools.partial(kernel, lat_count, lon_count), out_shape...]
where the time goes in v3:
time: 70.9 us; the launch traced here: 69.8 us
  Pallas kernels  69.2 us (98%)
    pallas_call x1, Pallas kernels, on_device(): pl.pallas_call(functools.partial(kernel, lat_count, lon_count), out_shape...  67.2 us
    pallas_call x1, Pallas kernels, on_device(): pl.pallas_call(unpack, out_shape=[jax.ShapeDtypeStruct(shape, F32) for sh...  2 us

profile of v3, /device:TPU:24, one launch (start us, length us, event | category | flops | bytes accessed | tf_op | source)
XLA Modules:
  0.0 69.8 jit_solution(10736124747588494240)
XLA Ops:
  0.6 67.2 %shard_map.161 = (f32[40,16,128]{2,1,0:T(8,128)}, f32[40,16,128]{2,1,0:T(8,128)}, f32[128,128]{1,0:T(8,128)}) custom-call(f32[40,16,128]{2,1,0:T(8,128)} %bitcast.12, s32[10,16,128]{2,1,0:T(8,128)} %mask.1, f32[16,128]{1,0:T(8,128)} %flux.1, f32[40,64]{1,0:T(8,128)} %win.1, f32[1,64]{1,0:T(1,128)} %bitcast.15, f32[64,64]{1,0:T(8,128)} %wmid.1, ...), custom_call_target="tpu_custom_call" | custom-call | tf_op jit(solution)/shard_map/pallas_call | solution.py:950
  67.8 2.0 %shard_map.162 = (f32[40,16,128]{2,1,0:T(8,128)}, f32[40,16,128]{2,1,0:T(8,128)}, f32[40,64]{1,0:T(8,128)}, f32[1,64]{1,0:T(1,128)}, f32[64,64]{1,0:T(8,128)}, /...) custom-call(f32[40,16,128]{2,1,0:T(8,128)} %get-tuple-element.19.fin, f32[40,16,128]{2,1,0:T(8,128)} %get-tuple-element.20.grad, ...), custom_call_target="tpu_custom_call" | custom-call | tf_op jit(solution)/shard_map/pallas_call | solution.py:1025

commit v4 on v3

--- a/solution.py
+++ b/solution.py
@@ -99,6 +99,19 @@
     wst_r,
     wc_s,
     wc_r,
+    t2h,
+    t1h,
+    t2s,
+    t1s,
+    tp,
+    tm,
+    sdx,
+    sdy,
+    pe24,
+    mw24,
+    acc24,
+    pnh,
+    mnh,
     h_send,
     h_recv,
     w_send,
@@ -323,15 +336,14 @@
         there = (lane >= 12 * l + 6) & (lane < 12 * l + 9)
         return jnp.where(here, low, jnp.where(there, high, strip))
 
-    def wide_stage(e, strips):
-        k = 3 * e
+    def wide_stage(e, strips, field_ref, top, count):
         for j in range(3):
-            wrow_s[e, 0, j, 0:FEAT] = take_rows(xs.at[k], 21 + j, PAD)
-            wrow_s[e, 1, j, 0:FEAT] = take_rows(xs.at[k], 8 + j, PAD)
+            wrow_s[e, 0, j, 0:FEAT] = take_rows(field_ref, top + 13 + j, count)
+            wrow_s[e, 1, j, 0:FEAT] = take_rows(field_ref, top + j, count)
             if e == 0:
                 wrow_s[e, 0, j, 40:48] = jnp.broadcast_to(depth_own[13 + j : 14 + j], (8, COLS))
                 wrow_s[e, 1, j, 40:48] = jnp.broadcast_to(depth_own[j : j + 1], (8, COLS))
-        if e == 1:
+        if e > 0:
             wc_s[e] = jnp.zeros((2, 16, COLS), F32)
         for f, strip in enumerate(strips):
             wst_s[e, f] = strip
@@ -347,26 +359,31 @@
 
     def wide_unpack(e):
         k = 3 * e
-        put_rows(xs.at[k], 7, PAD, wrow_r[e, 0, 2, 0:FEAT])
-        put_rows(xs.at[k], 24, PAD, wrow_r[e, 1, 0, 0:FEAT])
+        if e < 2:
+            put_rows(xs.at[k], 7, PAD, wrow_r[e, 0, 2, 0:FEAT])
+            put_rows(xs.at[k], 24, PAD, wrow_r[e, 1, 0, 0:FEAT])
+            own_ref, top, count, halo_ref = xs.at[k], 8, PAD, xh.at[k]
+        else:
+            own_ref, top, count, halo_ref = t2, 0, ROWS, t2h
         for j in range(3):
-            put_rows(xh.at[k], j, 8, wrow_r[e, 0, j, 0:FEAT])
-            put_rows(xh.at[k], 5 + j, 8, wrow_r[e, 1, j, 0:FEAT])
-        put_rows(xh.at[k], 3, 8, take_rows(xs.at[k], 8, PAD))
-        put_rows(xh.at[k], 4, 8, take_rows(xs.at[k], 23, PAD))
+            put_rows(halo_ref, j, 8, wrow_r[e, 0, j, 0:FEAT])
+            put_rows(halo_ref, 5 + j, 8, wrow_r[e, 1, j, 0:FEAT])
+        put_rows(halo_ref, 3, 8, take_rows(own_ref, top, count))
+        put_rows(halo_ref, 4, 8, take_rows(own_ref, top + 15, count))
         slots = slot[0:ROWS]
         below = pick(wc_r[e, 1], wc_r[e, 0], wc_r[e, 2], slots)
         above = pick(wc_r[e, 4], wc_r[e, 3], wc_r[e, 5], slots)
         for f in range(5 if e == 0 else 4):
             own = pick(wst_r[e, 0, f], wst_s[e, f], wst_r[e, 1, f], slots)
-            to = st.at[k, f] if f < 4 else sd
+            to = t2s.at[f] if e > 1 else (st.at[k, f] if f < 4 else sd)
             to[0:16, :] = own
             to[16:19, :] = below[3 * f : 3 * f + 3]
             to[19:20, :] = own[0:1]
             to[20:21, :] = own[15:16]
             to[21:24, :] = above[3 * f : 3 * f + 3]
         if e == 0:
-            dh[...] = jnp.zeros((8, COLS), F32)
+            dh[3:4] = depth_own[0:1]
+            dh[4:5] = depth_own[15:16]
             for j in range(3):
                 dh[j : j + 1] = wrow_r[e, 0, j, 40:41]
                 dh[5 + j : 6 + j] = wrow_r[e, 1, j, 40:41]
@@ -442,7 +459,7 @@
             strips[f] = strip_pack(strips[f], x, l)
         strips[4] = strip_pack(strips[4], depth_own, l)
     wc_s[0] = jnp.zeros((2, 16, COLS), F32)
-    wide_stage(0, strips)
+    wide_stage(0, strips, xs.at[0], 8, PAD)
 
     def stage_rows(e, north_ref, south_ref):
         row_s[e, 0] = take_rows(north_ref, 23, PAD)
@@ -465,18 +482,18 @@
 
     @pl.when(jnp.logical_not(has_s))
     def _():
-        for e in range(6):
+        for e in (0, 3):
             row_r[e, 0] = jnp.zeros((FEAT, COLS), F32)
-        for e in range(2):
+        for e in range(4):
             wrow_r[e, 0] = jnp.zeros((3, 48, COLS), F32)
             for d in range(3):
                 wc_r[e, d] = jnp.zeros((16, COLS), F32)
 
     @pl.when(jnp.logical_not(has_n))
     def _():
-        for e in range(6):
+        for e in (0, 3):
             row_r[e, 1] = jnp.zeros((FEAT, COLS), F32)
-        for e in range(2):
+        for e in range(4):
             wrow_r[e, 1] = jnp.zeros((3, 48, COLS), F32)
             for d in range(3, 6):
                 wc_r[e, d] = jnp.zeros((16, COLS), F32)
@@ -657,6 +674,8 @@
             d_y.append(north_q - south_q)
             sum_x.append(east_q + west_q)
             sum_y.append(north_q + south_q)
+            sdx[k, f] = d_x[f]
+            sdy[k, f] = d_y[f]
 
         def down(slope):
             total = GAIN_T * slope[0] + GAIN_S * slope[1]
@@ -723,7 +742,7 @@
                     south = jnp.concatenate([south, pltpu.roll(edge, 1, 0)], axis=0)
                 d_x = ew[k, fl, 0:tall]
                 d_y = north - south
-                ns[k, fl] = d_y[0:ROWS]
+                ns[k, fl, 0:tall] = d_y
                 if f < 2:
                     press_x = press_x + (GAIN_T, GAIN_S)[f] * d_x
                     press_y = press_y + (GAIN_T, GAIN_S)[f] * d_y
@@ -758,7 +777,7 @@
         if stage < 2:
             strip_section(k)
         elif k == 2:
-            wide_stage(1, strips)
+            wide_stage(1, strips, xs.at[3], 8, PAD)
             wide_launch(1)
 
     def give(n, source):
@@ -814,7 +833,7 @@
             along_x = along_y = blank
             for f in range(4):
                 along_x = along_x + g[f] * ew[k, f * LEV + l, 0:ROWS]
-                along_y = along_y + g[f] * ns[k, f * LEV + l]
+                along_y = along_y + g[f] * ns[k, f * LEV + l, 0:ROWS]
             to_u = cor * g[3] + hm * along_x
             to_v = cor * g[2] - 0.5 * along_y
             for f in range(4):
@@ -838,24 +857,126 @@
             odd_lane, pltpu.roll(col_r[e, 0], 1, 1), pltpu.roll(col_r[e, 1], COLS - 1, 1)
         )
 
-        def body(l, carry):
+        strips = [blank] * 4
+        for l in range(LEV):
             for f in range(4):
                 fl = f * LEV + l
                 turned = pltpu.roll(received, COLS - 1 - 2 * fl, 1)
                 got = acc[fl] + jnp.where(first_lane | last_lane, turned, 0.0)
-                if stage == 2:
-                    t2[fl] = (2.0 / 3.0) * source[fl] + got
-                elif stage == 1:
-                    t1[fl] = 0.25 * t2[fl] + got
-                else:
-                    new = (1.0 / 3.0) * source[fl] + 0.75 * t2[fl] + t1[fl] + got + dx[fl]
-                    if n == 5:
-                        grad[fl] = jnp.where(depth > l, new, 0.0)
-                    else:
-                        lam[fl] = new
-            return carry
-
-        levels(body, 0)
+                new = (2.0 / 3.0) * source[fl] + got
+                t2[fl] = new
+                strips[f] = strip_pack(strips[f], new, l)
+        w = 2 if n == 0 else 3
+        wide_stage(w, strips, t2, 0, ROWS)
+        wide_launch(w)
+
+    def far_adjoint(k, scale, own_ref, halo_ref, strip_ref, finish, spread):
+        deep = jnp.concatenate([depth_own, dh[...]], axis=0)
+        wet_s = (group.astype(F32) < sd[...]) & (lane24 < 12 * LEV)
+        gs = [jnp.where(wet_s, (DT * scale) * strip_ref[f], 0.0) for f in range(4)]
+
+        def up(total):
+            for hop in (12, 24, 48, 96):
+                later = pltpu.roll(total, COLS - hop, 1)
+                total = total + jnp.where(lane24 < COLS - hop, later, 0.0)
+            return total
+
+        def parts(f, g, u, v, sum_u, sum_v):
+            a = (u * hm24) * g
+            b = (v * 0.5) * g
+            if f < 2:
+                a = a + (GAIN_T, GAIN_S)[f] * (hm24 * sum_u)
+                b = b + (GAIN_T, GAIN_S)[f] * (0.5 * sum_v)
+            base = (MIX[f] * cc24) * g
+            flat = MIX[f] * g
+            return base + a, base - a, flat + b, flat - b
+
+        def local(g, slopes_x, slopes_y):
+            along_x = along_y = jnp.zeros((TALL, COLS), F32)
+            for f in range(4):
+                along_x = along_x + g[f] * slopes_x[f]
+                along_y = along_y + g[f] * slopes_y[f]
+            given = [-2.0 * (MIX[f] * cc24 + MIX[f]) * g[f] for f in range(4)]
+            given[2] = given[2] - (cor24 * g[3] + hm24 * along_x)
+            given[3] = given[3] + (cor24 * g[2] - 0.5 * along_y)
+            return given
+
+        up_u, up_v = up(gs[2]), up(gs[3])
+        side = [parts(f, gs[f], st[k, 2], st[k, 3], up_u, up_v) for f in range(4)]
+        if spread:
+            given = local(gs, [sdx[k, f] for f in range(4)], [sdy[k, f] for f in range(4)])
+            for f in range(4):
+                plus, minus, to_s, to_n = side[f]
+                north_s, _ = rise(to_s[0:16], to_s[16:24])
+                _, south_s = rise(to_n[0:16], to_n[16:24])
+                new = scale * strip_ref[f] + given[f] + north_s + south_s
+                new = new + pltpu.roll(plus, COLS - 1, 1) + pltpu.roll(minus, 1, 1)
+                t1s[f, 0:16, :] = new[0:16]
+                t1s[f, 16:24, :] = mend(new[16:24], new[0:16])
+        for f in range(4):
+            tp[f] = side[f][0]
+            tm[f] = side[f][1]
+
+        sum_u = sum_v = jnp.zeros((TALL, COLS), F32)
+        for l in range(LEV - 1, -1, -1):
+            wet = deep > float(l)
+            at = [f * LEV + l for f in range(4)]
+            g = []
+            for fl in at:
+                x = jnp.concatenate([own_ref[fl], halo_ref[fl]], axis=0)
+                g.append(jnp.where(wet, (DT * scale) * x, 0.0))
+            sum_u = sum_u + g[2]
+            sum_v = sum_v + g[3]
+            u = jnp.concatenate([xs[k, at[2], 8:24, :], xh[k, at[2]]], axis=0)
+            v = jnp.concatenate([xs[k, at[3], 8:24, :], xh[k, at[3]]], axis=0)
+            given = local(g, [ew[k, fl] for fl in at], [ns[k, fl] for fl in at])
+            for f, fl in enumerate(at):
+                plus, minus, to_s, to_n = parts(f, g[f], u, v, sum_u, sum_v)
+                pe24[fl] = plus
+                mw24[fl] = minus
+                acc24[fl] = given[f]
+                pn[fl, 8:24, :] = to_s[0:16]
+                mn[fl, 8:24, :] = to_n[0:16]
+                pn[fl, 24:25, :] = to_s[21:22]
+                mn[fl, 7:8, :] = to_n[18:19]
+                pnh[fl] = to_s[16:24]
+                mnh[fl] = to_n[16:24]
+        first24, last24 = lane24 == 0, lane24 == COLS - 1
+        for l in range(LEV):
+            for f in range(4):
+                fl = f * LEV + l
+                from_w = pltpu.roll(tm[f], (2 * COLS - 2 - 12 * l) % COLS, 1)
+                from_e = pltpu.roll(tp[f], (2 * COLS - 10 - 12 * l) % COLS, 1)
+                w_side = jnp.where(first24, from_w, pltpu.roll(mw24[fl], 1, 1))
+                e_side = jnp.where(last24, from_e, pltpu.roll(pe24[fl], COLS - 1, 1))
+                got = acc24[fl] + w_side + e_side
+                own = got[0:16] + pn[fl, 9:25, :] + mn[fl, 7:23, :]
+                edge = None
+                if spread:
+                    edge = got[16:24] + pltpu.roll(pnh[fl], 7, 0) + pltpu.roll(mnh[fl], 1, 0)
+                finish(fl, l, own, edge)
+
+    def back_two(e, source):
+        k = 3 * (3 - e)
+
+        def middle(fl, l, own, edge):
+            new = 0.25 * t2[fl] + own
+            t1[fl] = new
+            t1h[fl] = mend(0.25 * t2h[fl] + edge, new)
+
+        def start(fl, l, own, edge):
+            new = (1.0 / 3.0) * source[fl] + 0.75 * t2[fl] + t1[fl] + own + dx[fl]
+            if k == 0:
+                grad[fl] = jnp.where(depth > l, new, 0.0)
+            else:
+                lam[fl] = new
+
+        wide_unpack(e)
+        far_adjoint(k + 1, 0.25, t2, t2h, t2s, middle, True)
+        far_adjoint(k, 1.0, t1, t1h, t1s, start, False)
+        if k > 0:
+            put_rows(mn, 7, PAD, jnp.zeros((FEAT, COLS), F32))
+            put_rows(pn, 24, PAD, jnp.zeros((FEAT, COLS), F32))
 
     prepare()
     layer_one(0)
@@ -886,38 +1007,30 @@
     forward(5, forcing)
     keep(0, cot)
     take(0, cot)
-    give(1, t2)
-    keep(1, t2)
     weight_grads(1, False)
-    take(1, cot)
-    give(2, t1)
-    keep(2, t1)
-    take(2, cot)
+    wide_arrive(2)
+    back_two(2, cot)
     give(3, lam)
     keep(3, lam)
     back_out(0, lam)
     back_mid(0)
-    take(3, lam)
-    give(4, t2)
-    keep(4, t2)
     weight_grads(0, True)
     fan_start(2)
     back_in(0)
-    take(4, lam)
-    give(5, t1)
-    keep(5, t1)
+    take(3, lam)
     fan_arrive(2)
     c1[...] = slot_sum(2, gb[part(spot)], rs1)
     fan_start(3)
-    take(5, lam)
+    wide_arrive(3)
     fan_arrive(3)
     scale = 1.0 / math.sqrt(lat_count * ROWS * lon_count * COLS)
     c2[...] = slot_sum(3, c1[...], rs2) * scale
     ag[part(spot)] = c2[...]
     fan_start(4)
-    for e in range(6):
+    back_two(3, lam)
+    for e in (0, 3):
         drain(e)
-    for e in range(2):
+    for e in range(4):
         wide_drain(e)
     for stage in range(4):
         fan_drain(stage)
@@ -956,7 +1069,7 @@
             v(6, *tall),
             v(FEAT, TALL, COLS),
             v(6, FEAT, TALL, COLS),
-            v(6, *field),
+            v(6, FEAT, TALL, COLS),
             v(*field),
             v(*field),
             v(*tall),
@@ -994,16 +1107,29 @@
             v(6, 4, TALL, COLS),
             v(TALL, COLS),
             v(8, COLS),
-            v(2, 2, 3, 48, COLS),
-            v(2, 2, 3, 48, COLS),
-            v(2, 5, ROWS, COLS),
-            v(2, 2, 5, ROWS, COLS),
-            v(2, 2, 16, COLS),
-            v(2, 6, 16, COLS),
+            v(4, 2, 3, 48, COLS),
+            v(4, 2, 3, 48, COLS),
+            v(4, 5, ROWS, COLS),
+            v(4, 2, 5, ROWS, COLS),
+            v(4, 2, 16, COLS),
+            v(4, 6, 16, COLS),
+            v(FEAT, 8, COLS),
+            v(FEAT, 8, COLS),
+            v(4, TALL, COLS),
+            v(4, TALL, COLS),
+            v(4, TALL, COLS),
+            v(4, TALL, COLS),
+            v(6, 4, TALL, COLS),
+            v(6, 4, TALL, COLS),
+            v(FEAT, TALL, COLS),
+            v(FEAT, TALL, COLS),
+            v(FEAT, TALL, COLS),
+            v(FEAT, 8, COLS),
+            v(FEAT, 8, COLS),
             pltpu.SemaphoreType.DMA((6, 4)),
             pltpu.SemaphoreType.DMA((6, 4)),
-            pltpu.SemaphoreType.DMA((2, 10)),
-            pltpu.SemaphoreType.DMA((2, 10)),
+            pltpu.SemaphoreType.DMA((4, 10)),
+            pltpu.SemaphoreType.DMA((4, 10)),
             pltpu.SemaphoreType.DMA((5, max(near, far))),
             pltpu.SemaphoreType.DMA((5, max(near, far))),
         ],

time: 70.9 us -> 64.6 us (0.911)
  Pallas kernels: 69.2 us -> 62.7 us
    pallas_call x1, Pallas kernels: 67.2 us -> 60.7 us  [on_device(): pl.pallas_call(functools.partial(kernel, lat_count, lon_count), out_shape...]
where the time goes in v4:
time: 64.6 us; the launch traced here: 63.3 us
  Pallas kernels  62.7 us (97%)
    pallas_call x1, Pallas kernels, on_device(): pl.pallas_call(functools.partial(kernel, lat_count, lon_count), out_shape...  60.7 us
    pallas_call x1, Pallas kernels, on_device(): pl.pallas_call(unpack, out_shape=[jax.ShapeDtypeStruct(shape, F32) for sh...  2 us

profile of v4, /device:TPU:24, one launch (start us, length us, event | category | flops | bytes accessed | tf_op | source)
XLA Modules:
  0.0 63.3 jit_solution(11247683666135794977)
XLA Ops:
  0.6 60.7 %shard_map.161 = (f32[40,16,128]{2,1,0:T(8,128)}, f32[40,16,128]{2,1,0:T(8,128)}, f32[128,128]{1,0:T(8,128)}) custom-call(f32[40,16,128]{2,1,0:T(8,128)} %bitcast.12, s32[10,16,128]{2,1,0:T(8,128)} %mask.1, f32[16,128]{1,0:T(8,128)} %flux.1, f32[40,64]{1,0:T(8,128)} %win.1, f32[1,64]{1,0:T(1,128)} %bitcast.15, f32[64,64]{1,0:T(8,128)} %wmid.1, ...), custom_call_target="tpu_custom_call" | custom-call | tf_op jit(solution)/shard_map/pallas_call | solution.py:1063
  61.3 2.0 %shard_map.162 = (f32[40,16,128]{2,1,0:T(8,128)}, f32[40,16,128]{2,1,0:T(8,128)}, f32[40,64]{1,0:T(8,128)}, f32[1,64]{1,0:T(1,128)}, f32[64,64]{1,0:T(8,128)}, /...) custom-call(f32[40,16,128]{2,1,0:T(8,128)} %get-tuple-element.19.fin, f32[40,16,128]{2,1,0:T(8,128)} %get-tuple-element.20.grad, ...), custom_call_target="tpu_custom_call" | custom-call | tf_op jit(solution)/shard_map/pallas_call | solution.py:1151
